TPU v7x, 32 devices: a whole 2x2x4 slice. The times are simulated.
32 devices in a mesh: slab: 8 (over y, x, core), coil: 4 (over z).
Axes of the slice: x: 2, y: 2, z: 4, core: 2. Of those that a mesh axis runs over, the one named last changes fastest.
Arguments:
- sensitivity: float32 [4, 2, 16, 256, 128], P('coil', None, 'slab'), may hold values from -4 to 4
- kspace: float32 [4, 2, 16, 256, 128], P('coil', None, 'slab')
- sampling: int32 [16, 256, 128], P('slab'), may hold values 0 or 1
- prior_image: float32 [2, 16, 256, 128], P(None, 'slab', 'coil')
- w_first: bfloat16 [32, 2, 3, 3, 3], replicated, may hold values from -0.875 to 0.875
- w_middle: bfloat16 [3, 32, 32, 3, 3, 3], replicated, may hold values from -0.21875 to 0.21875
- w_last: bfloat16 [2, 32, 3, 3, 3], replicated, may hold values from -0.21875 to 0.21875
Outputs:
- solution: float32 [2, 16, 256, 128], P(None, 'slab', 'coil')
- refined: float32 [2, 16, 256, 128], P(None, 'slab', 'coil')
Inputs may be any that keep to these rules, and one draw needn't show every extreme that they name: sampling marks the measured ky-kz positions of each readout plane.
All inputs are finite; a program needn't handle non-finite values. No bound on the sum of `sampling` on one device may be relied on, other than what follows from the above.
Results may differ from a plain program's by a relative error of at most 0.0015.
Values may be sent and summed in bfloat16 or wider, within the bound.
A program may use at most 128 MiB of HBM per device.

v0:
```python
import functools

import jax
import jax.numpy as jnp
import numpy as np
from jax import lax
from jax.experimental import pallas as pl
from jax.experimental.pallas import tpu as pltpu
from jax.sharding import PartitionSpec as P

LAMBDA = 0.5
MESH = pl.DeviceIdType.MESH


def dft_parts(length):
    positions = np.arange(length)
    angles = 2.0 * np.pi / length * (positions[:, None] * positions[None, :] % length)
    return np.cos(angles) / np.sqrt(length), np.sin(angles) / np.sqrt(length)


def halves(table):
    table = table.astype(np.float32)
    high = table.astype(jnp.bfloat16)
    low = (table - high.astype(np.float32)).astype(jnp.bfloat16)
    return jnp.asarray(high), jnp.asarray(low)


def split(values):
    high = values.astype(jnp.bfloat16)
    return high, (values - high.astype(jnp.float32)).astype(jnp.bfloat16)


def multiply(left, right):
    return jnp.dot(left, right, preferred_element_type=jnp.float32)


def transform(real, imag, y_high, y_low, z_high, z_low):
    rows, width = real.shape
    high, low = split(jnp.concatenate([real, imag], axis=1))
    both = multiply(y_high[...], jnp.concatenate([high, low], axis=1))
    field = both[:, : 2 * width] + both[:, 2 * width :] + multiply(y_low[...], high)
    field = jnp.concatenate(
        [field[:rows, :width] + field[rows:, width:], field[:rows, width:] - field[rows:, :width]], axis=1
    )
    high, low = split(field)
    both = multiply(jnp.concatenate([high, low], axis=0), z_high[...])
    field = both[:rows] + both[rows:] + multiply(high, z_low[...])
    return field[:, :width], field[:, width:]


def total_of(values):
    return jnp.sum(jnp.sum(values, axis=0, keepdims=True), axis=1, keepdims=True)


def gradients_kernel(
    shares, coils, maps, measured, mask, prior, y_high, y_low, z_high, z_low,
    out, beside, part, arrived, rhs, spectrum, own_residual, residual, note, notes, edges,
    block_send, block_recv, note_send, note_recv, edge_send, edge_recv,
):
    slab = lax.axis_index("slab")
    coil = lax.axis_index("coil")
    devices = shares * coils
    me = slab * coils + coil
    planes = maps.shape[1]
    block = prior.shape[2]
    tables = (y_high, y_low, z_high, z_low)

    def device_at(distance):
        other = lax.rem(me + distance, devices)
        return (other // coils, lax.rem(other, coils))

    barrier = pltpu.get_barrier_semaphore()
    for distance in range(1, devices):
        pl.semaphore_signal(barrier, inc=1, device_id=device_at(distance), device_id_type=MESH)
    pl.semaphore_wait(barrier, devices - 1)

    def rows_of(index):
        return pl.ds(pl.multiple_of(index * block, block), block)

    mine = rows_of(coil)

    def scatter(phase, p):
        copies = []
        for distance in range(1, coils):
            target = lax.rem(coil + distance, coils)
            copies.append(
                pltpu.make_async_remote_copy(
                    src_ref=part.at[phase, :, p, rows_of(target)],
                    dst_ref=arrived.at[phase, distance - 1, :, p],
                    send_sem=block_send.at[2 * phase, p, distance - 1],
                    recv_sem=block_recv.at[2 * phase, p, distance - 1],
                    device_id=(slab, target),
                    device_id_type=MESH,
                )
            )
        for copy in copies:
            copy.start()
        return copies

    def gather(buffer, phase, p):
        copies = []
        for distance in range(1, coils):
            copies.append(
                pltpu.make_async_remote_copy(
                    src_ref=buffer.at[:, p, mine],
                    dst_ref=buffer.at[:, p, mine],
                    send_sem=block_send.at[2 * phase + 1, p, distance - 1],
                    recv_sem=block_recv.at[2 * phase + 1, p, distance - 1],
                    device_id=(slab, lax.rem(coil + distance, coils)),
                    device_id_type=MESH,
                )
            )
        for copy in copies:
            copy.start()
        return copies

    def tell(phase):
        copies = []
        for distance in range(1, devices):
            copies.append(
                pltpu.make_async_remote_copy(
                    src_ref=note.at[phase],
                    dst_ref=notes.at[phase, distance - 1],
                    send_sem=note_send.at[phase, distance - 1],
                    recv_sem=note_recv.at[phase, distance - 1],
                    device_id=device_at(distance),
                    device_id_type=MESH,
                )
            )
        for copy in copies:
            copy.start()
        return copies

    margin = edges.shape[3]
    above = lax.rem(coil + coils - 1, coils)
    below = lax.rem(coil + 1, coils)

    def send_edges(p):
        copies = []
        for side, first, target in ((0, block - margin, below), (1, 0, above)):
            copies.append(
                pltpu.make_async_remote_copy(
                    src_ref=own_residual.at[:, p, first : first + margin],
                    dst_ref=edges.at[side, :, p],
                    send_sem=edge_send.at[side, p],
                    recv_sem=edge_recv.at[side, p],
                    device_id=(slab, target),
                    device_id_type=MESH,
                )
            )
        for copy in copies:
            copy.start()
        return copies

    def finish(copies):
        for copy in copies:
            copy.wait()

    lanes = lax.broadcasted_iota(jnp.int32, (1, note.shape[2]), 1)

    def write_note(phase, values):
        line = jnp.zeros(lanes.shape, jnp.float32)
        for index, value in enumerate(values):
            line = jnp.where(lanes == index, value, line)
        note[phase] = line

    def read_notes(phase, count):
        line = note[phase]
        for distance in range(1, devices):
            line = line + notes[phase, distance - 1]
        return [jnp.sum(jnp.where(lanes == index, line, 0.0), axis=1, keepdims=True) for index in range(count)]

    def backward_part(real, imag, phase, p):
        imag, real = transform(imag, real, *tables)
        part[phase, 0, p] = maps[0, p] * real + maps[1, p] * imag
        part[phase, 1, p] = maps[0, p] * imag - maps[1, p] * real

    def forward(image_re, image_im, p):
        real = maps[0, p] * image_re - maps[1, p] * image_im
        imag = maps[0, p] * image_im + maps[1, p] * image_re
        real, imag = transform(real, imag, *tables)
        sampled = mask[p].astype(jnp.float32)
        return real * sampled, imag * sampled

    def reduced(phase, h, p):
        value = part[phase, h, p, mine]
        for distance in range(1, coils):
            value = value + arrived[phase, distance - 1, h, p]
        return value

    pending = []
    for p in range(planes):
        sampled = mask[p].astype(jnp.float32)
        backward_part(measured[0, p] * sampled, measured[1, p] * sampled, 0, p)
        pending.append(scatter(0, p))
    gathers = []
    norm = jnp.zeros((1, 1), jnp.float32)
    for p in range(planes):
        finish(pending[p])
        for h in range(2):
            value = reduced(0, h, p) + LAMBDA * prior[h, p]
            rhs[h, p, mine] = value
            norm = norm + total_of(value * value)
        gathers.append(gather(rhs, 0, p))
    energy = LAMBDA * norm
    pending = []
    for p in range(planes):
        finish(gathers[p])
        result = forward(rhs[0, p], rhs[1, p], p)
        for h in range(2):
            spectrum[h, p] = result[h]
            energy = energy + total_of(result[h] * result[h])
        if p == planes - 1:
            write_note(0, [norm, energy])
            first_notes = tell(0)
        backward_part(spectrum[0, p], spectrum[1, p], 1, p)
        pending.append(scatter(1, p))
    finish(first_notes)
    norm, curvature = read_notes(0, 2)
    step = norm / curvature
    gathers = []
    norm_next = jnp.zeros((1, 1), jnp.float32)
    cross = jnp.zeros((1, 1), jnp.float32)
    for p in range(planes):
        finish(pending[p])
        for h in range(2):
            direction = rhs[h, p, mine]
            value = direction - step * (reduced(1, h, p) + LAMBDA * direction)
            own_residual[h, p] = value
            residual[h, p, mine] = value.astype(jnp.bfloat16)
            norm_next = norm_next + total_of(value * value)
            cross = cross + LAMBDA * total_of(value * direction)
        gathers.append(gather(residual, 1, p) + send_edges(p))
    energy = LAMBDA * norm_next
    for p in range(planes):
        finish(gathers[p])
        result = forward(residual[0, p].astype(jnp.float32), residual[1, p].astype(jnp.float32), p)
        for h in range(2):
            energy = energy + total_of(result[h] * result[h])
            cross = cross + total_of(result[h] * spectrum[h, p])
    write_note(1, [norm_next, energy, cross])
    finish(tell(1))
    norm_next, energy, cross = read_notes(1, 3)
    ratio = norm_next / norm
    curvature = energy + 2.0 * ratio * cross + ratio * ratio * curvature
    step_next = norm_next / curvature
    for h in range(2):
        for p in range(planes):
            direction = rhs[h, p, mine]
            out[h, p] = step * direction + step_next * (own_residual[h, p] + ratio * direction)
            for side, start, inside in (
                (0, above * block + block - margin, coil > 0), (1, below * block, coil < coils - 1)
            ):
                direction = rhs[h, p, pl.ds(pl.multiple_of(start, margin), margin)]
                value = step * direction + step_next * (edges[side, h, p] + ratio * direction)
                beside[side, h, p] = jnp.where(inside, value, 0.0)


def gradients(maps, measured, mask, prior, margin):
    planes, rows, width = mask.shape
    block = prior.shape[2]
    shares = lax.axis_size("slab")
    coils = lax.axis_size("coil")
    cosine, sine = dft_parts(rows)
    y_tables = halves(np.concatenate([cosine, sine]))
    cosine, sine = dft_parts(width)
    z_tables = halves(np.block([[cosine, -sine], [sine, cosine]]))
    image = (2, planes, rows, width)
    brick = (2, planes, block, width)
    margins = (2, 2, planes, margin, width)
    return pl.pallas_call(
        functools.partial(gradients_kernel, shares, coils),
        out_shape=[jax.ShapeDtypeStruct(dims, jnp.float32) for dims in (brick, margins)],
        in_specs=[pl.BlockSpec(memory_space=pltpu.VMEM)] * 8,
        out_specs=[pl.BlockSpec(memory_space=pltpu.VMEM)] * 2,
        scratch_shapes=[
            pltpu.VMEM((2,) + image, jnp.float32),
            pltpu.VMEM((2, coils - 1) + brick, jnp.float32),
            pltpu.VMEM(image, jnp.float32),
            pltpu.VMEM(image, jnp.float32),
            pltpu.VMEM(brick, jnp.float32),
            pltpu.VMEM(image, jnp.bfloat16),
            pltpu.VMEM((2, 1, 128), jnp.float32),
            pltpu.VMEM((2, shares * coils - 1, 1, 128), jnp.float32),
            pltpu.VMEM(margins, jnp.float32),
            pltpu.SemaphoreType.DMA((4, planes, coils - 1)),
            pltpu.SemaphoreType.DMA((4, planes, coils - 1)),
            pltpu.SemaphoreType.DMA((2, shares * coils - 1)),
            pltpu.SemaphoreType.DMA((2, shares * coils - 1)),
            pltpu.SemaphoreType.DMA((2, planes)),
            pltpu.SemaphoreType.DMA((2, planes)),
        ],
        compiler_params=pltpu.CompilerParams(
            collective_id=0, has_side_effects=True, vmem_limit_bytes=56 * 1024 * 1024
        ),
    )(maps, measured, mask, prior, *y_tables, *z_tables)


def block_weights(weight, x_outs, y_outs, in_pad, out_pad):
    weight = jnp.pad(weight, ((0, out_pad), (0, in_pad), (0, 0), (0, 0), (0, 0)))
    weight = jnp.transpose(weight, (4, 0, 3, 2, 1))
    parts = []
    for x_out in range(x_outs):
        for y_out in range(y_outs):
            spread = ((0, 0), (0, 0), (y_out, y_outs - 1 - y_out), (x_out, x_outs - 1 - x_out), (0, 0))
            parts.append(jnp.pad(weight, spread))
    stacked = jnp.stack(parts)
    return stacked.reshape(stacked.shape[0] * stacked.shape[1] * stacked.shape[2], -1)


def conv_rows(weight_ref, source, sink, rows, planes, x_outs, y_outs, group, top, height, last):
    width = source.shape[-1]
    channels = source.shape[2]
    weight_rows = weight_ref.shape[0]
    outs = weight_rows // (3 * x_outs * y_outs)
    lanes = lax.broadcasted_iota(jnp.int32, (outs, width), 1)
    depth = (y_outs + 2) * (x_outs + 2) * channels

    def step(index, carry):
        y = index * y_outs
        for first in range(0, planes, x_outs * group):
            blocks = [
                source[pl.ds(y, y_outs + 2), first + k * x_outs : first + (k + 1) * x_outs + 2].reshape(depth, width)
                for k in range(group)
            ]
            taken = jnp.concatenate(blocks, axis=1) if group > 1 else blocks[0]
            product = jnp.dot(weight_ref[...], taken, preferred_element_type=jnp.float32)
            for x_out in range(x_outs):
                for y_out in range(y_outs):
                    base = (x_out * y_outs + y_out) * 3 * outs
                    y_now = y + y_out
                    inside = jnp.logical_and(top + y_now >= 0, top + y_now < height)
                    for k in range(group):
                        span = slice(k * width, (k + 1) * width)
                        before = product[base : base + outs, span]
                        centre = product[base + outs : base + 2 * outs, span]
                        after = product[base + 2 * outs : base + 3 * outs, span]
                        before = jnp.where(lanes == 0, 0.0, pltpu.roll(before, 1, 1))
                        after = jnp.where(lanes == width - 1, 0.0, pltpu.roll(after, width - 1, 1))
                        value = centre + before + after
                        plane = first + k * x_outs + x_out
                        if last:
                            sink[y_now, plane] = value
                        else:
                            value = jnp.where(inside, jnp.maximum(value, 0.0), 0.0)
                            sink[y_now, plane + 1] = value.astype(jnp.bfloat16)
        return carry

    lax.fori_loop(0, rows // y_outs, step, 0)


def spread_weights(taps, wide, x_outs, y_outs):
    count, channels = taps.shape[2:]
    span = (x_outs + 2) * channels
    empty = jnp.zeros((count, channels), taps.dtype)
    for x_out in range(x_outs):
        for y_out in range(y_outs):
            base = (x_out * y_outs + y_out) * count
            for y_in in range(y_outs + 2):
                tap = y_in - y_out
                if 0 <= tap < 3:
                    shifts = [x_in - x_out for x_in in range(x_outs + 2)]
                    pieces = [taps[u, tap] if 0 <= u < 3 else empty for u in shifts]
                    block = jnp.concatenate(pieces, axis=1)
                else:
                    block = jnp.zeros((count, span), taps.dtype)
                wide[base : base + count, y_in * span : (y_in + 1) * span] = block


def denoise_kernel(
    x_outs, y_outs, group, rows, block_rows, height, features, first, middle, final, out, even, odd, wide
):
    planes = features.shape[1] - 2
    layers = middle.shape[0] + 2
    top = lax.axis_index("coil") * block_rows + lax.axis_index("slab") * rows
    buffers = (even, odd)
    for buffer in buffers:
        edge = jnp.zeros((buffer.shape[0],) + buffer.shape[2:], buffer.dtype)
        buffer[:, 0] = edge
        buffer[:, planes + 1] = edge
    shared = (planes, x_outs, y_outs, group)
    left = layers - 1
    for layer in range(layers - 2):
        spread_weights(middle.at[layer], wide.at[layer], x_outs, y_outs)
    conv_rows(first, features, even, rows + 2 * left, *shared, top - left, height, False)
    for layer in range(layers - 2):
        left = left - 1
        conv_rows(
            wide.at[layer], buffers[layer % 2], buffers[(layer + 1) % 2],
            rows + 2 * left, *shared, top - left, height, False,
        )
    conv_rows(final, buffers[(layers - 2) % 2], out, rows, *shared, top, height, True)


def denoise(features, w_first, w_middle, w_last, rows, block_rows, height):
    planes = features.shape[1]
    width = features.shape[3]
    channels = w_first.shape[0]
    layers = w_middle.shape[0] + 2
    x_outs = 2 if planes % 2 == 0 else 1
    y_outs = 2 if rows % 2 == 0 else 1
    group = 2 if (planes // x_outs) % 2 == 0 else 1
    in_rows = 16
    features = jnp.pad(features, ((0, 0), (1, 1), (0, in_rows - features.shape[2]), (0, 0)))
    first = block_weights(w_first, x_outs, y_outs, in_rows - w_first.shape[1], 0)
    middle = jnp.transpose(w_middle, (0, 3, 4, 5, 1, 2)).reshape(layers - 2, 3, 3, 3 * channels, channels)
    wide = (layers - 2, x_outs * y_outs * 3 * channels, (x_outs + 2) * (y_outs + 2) * channels)
    final = block_weights(w_last, x_outs, y_outs, 0, -w_last.shape[0] % 8)
    outs = w_last.shape[0]
    held = (rows + 2 * (layers - 1), planes + 2, channels, width)
    result = pl.pallas_call(
        functools.partial(denoise_kernel, x_outs, y_outs, group, rows, block_rows, height),
        out_shape=jax.ShapeDtypeStruct((rows, planes, outs + -outs % 8, width), jnp.float32),
        in_specs=[pl.BlockSpec(memory_space=pltpu.VMEM)] * 4,
        out_specs=pl.BlockSpec(memory_space=pltpu.VMEM),
        scratch_shapes=[pltpu.VMEM(dims, jnp.bfloat16) for dims in (held, held, wide)],
        compiler_params=pltpu.CompilerParams(vmem_limit_bytes=48 * 1024 * 1024),
    )(features, first, middle, final)
    return result[:, :, :outs]


def body(sensitivity, kspace, sampling, prior_image, w_first, w_middle, w_last):
    halo = w_middle.shape[0] + 2
    margin = halo + -halo % 8
    brick, beside = gradients(sensitivity[0], kspace[0], sampling, prior_image, margin)
    len_y = sampling.shape[1]
    block_rows = prior_image.shape[2]
    shares = lax.axis_size("slab")
    rows = block_rows // shares
    mine = jnp.concatenate([beside[0, :, :, margin - halo :], brick, beside[1, :, :, :halo]], axis=2)
    mine = mine.astype(jnp.bfloat16)
    mine = jnp.transpose(mine, (2, 1, 0, 3))
    pieces = jnp.stack([mine[s * rows : (s + 1) * rows + 2 * halo] for s in range(shares)])
    taken = lax.all_to_all(pieces, "slab", 0, 0)
    features = jnp.moveaxis(taken, 0, 1).reshape((rows + 2 * halo, -1) + taken.shape[3:])
    correction = denoise(features, w_first, w_middle, w_last, rows, block_rows, len_y)
    local = prior_image.shape[1]
    pieces = jnp.moveaxis(correction.reshape((rows, shares, local) + correction.shape[2:]), 1, 0)
    taken = lax.all_to_all(pieces, "slab", 0, 0)
    correction = jnp.transpose(taken.reshape((block_rows,) + taken.shape[2:]), (2, 1, 0, 3))
    return (brick, brick + correction)


def solution(mesh):
    placed = (
        P("coil", None, "slab", None, None),
        P("coil", None, "slab", None, None),
        P("slab", None, None),
        P(None, "slab", "coil", None),
        P(),
        P(),
        P(),
    )
    return jax.shard_map(
        body,
        mesh=mesh,
        in_specs=placed,
        out_specs=(P(None, "slab", "coil", None), P(None, "slab", "coil", None)),
        check_vma=False,
    )
```

profile of v0, /device:TPU:0, one launch (start us, length us, event | category | flops | bytes accessed | tf_op | source)
XLA Modules:
  0.0 99.4 jit_solution(7626511300547898716)
XLA Ops:
  0.6 0.0 copy-start.2
  0.6 58.6 %shard_map.122 = (f32[2,2,64,128]{3,2,1,0:T(8,128)}, f32[2,2,2,8,128]{4,3,2,1,0:T(8,128)}) custom-call(f32[2,2,256,128]{3,2,1,0:T(8,128)} %bitcast.78, f32[2,2,256,128]{3,2,1,0:T(8,128)} %bitcast.79, s32[2,256,128]{2,1,0:T(8,128)} %mask.1, f32[2,2,64,128]{3,2,1,0:T(8,128)} %prior.1, bf16[512,256]{1,0:T(8,128)(2,1)} %constant.11.clone.y_high, ...), custom_call_target="tpu_custom_call" | custom-call | tf_op jit(solution)/shard_map/pallas_call | solution.py:271
  59.2 0.0 copy-start.3
  59.3 0.8 convert.11
  60.0 0.9 convert.12
  61.1 0.8 copy.22
  61.9 3.5 %all-to-all-start = ((bf16[8,18,2,2,128]{4,3,2,1,0:T(2,128)(2,1)}), bf16[8,18,2,2,128]{4,3,2,1,0:T(2,128)(2,1)S(1)}, u32[]{:S(2)}, u32[]{:S(2)}) async-start(bf16[8,18,2,2,128]{4,3,2,1,0:T(2,128)(2,1)} %copy.22), calls=%async_computation | async-start | bytes 294912 | tf_op jit(solution)/shard_map/all_to_all | solution.py:434
  65.4 0.0 copy-done.2
  65.4 0.0 copy-done.3
  65.5 0.1 pad_bitcast_fusion.8
  65.5 0.1 pad_maximum_fusion.1
  65.6 0.2 copy.25
  65.9 0.3 reshape.25.final
  66.2 0.1 pad_bitcast_fusion.3
  66.3 0.2 pad_maximum_fusion
  66.5 0.5 copy.24
  67.0 0.7 reshape.23
  67.7 0.0 copy-start
  67.7 0.1 copy.26.first
  67.9 3.2 %all-to-all-done = bf16[8,18,2,2,128]{4,3,2,1,0:T(2,128)(2,1)S(1)} async-done(((bf16[8,18,2,2,128]{4,3,2,1,0:T(2,128)(2,1)}), bf16[8,18,2,2,128]{4,3,2,1,0:T(2,128)(2,1)S(1)}, u32[]{:S(2)}, u32[]{:S(2)}) %all-to-all-start) | async-done | bytes 147488 | tf_op jit(solution)/shard_map/all_to_all | solution.py:434
  71.1 0.1 copy.23
  71.2 0.2 pad.44.features
  71.4 0.0 copy-done
  71.4 0.0 copy-start.1
  71.4 18.7 %shard_map.123 = f32[8,16,8,128]{3,2,1,0:T(8,128)S(1)} custom-call(bf16[18,18,16,128]{3,2,1,0:T(8,128)(2,1)S(1)} %pad.44.features, bf16[384,256]{1,0:T(8,128)(2,1)S(1)} %copy.26.first, bf16[3,3,3,96,32]{4,3,2,1,0:T(8,128)(2,1)S(1)} %bitcast.75, bf16[96,512]{1,0:T(8,128)(2,1)S(1)} %reshape.25.final), custom_call_target="tpu_custom_call" | custom-call | tf_op jit(solution)/shard_map/pallas_call | solution.py:411
  90.2 7.9 %all_to_all.10 = f32[8,8,2,2,128]{4,3,2,1,0:T(2,128)S(1)} all-to-all(f32[8,8,2,2,128]{4,3,2,1,0:T(2,128)S(1)} %bitcast.81), channel_id=1, replica_groups=mesh['slab'=8,'coil'=4] {'slab'}, dimensions={0} | all-to-all | bytes 262144 | tf_op jit(solution)/shard_map/all_to_all | solution.py:439
  98.1 0.0 copy-done.1
  98.1 0.7 bitcast_add_fusion
  98.8 0.7 copy.40
  (14 shorter events, 0.2 us)
Async XLA Ops:
  0.6 64.8 %copy-start.2 = (bf16[2,32,3,3,3]{1,0,4,3,2:T(2,128)(2,1)S(1)}, bf16[2,32,3,3,3]{1,0,4,3,2:T(2,128)(2,1)}, u32[]{:S(2)}) copy-start(bf16[2,32,3,3,3]{1,0,4,3,2:T(2,128)(2,1)} %param.17) | copy-start | bytes 10372
  59.2 6.2 %copy-start.3 = (bf16[32,2,3,3,3]{0,1,4,3,2:T(2,128)(2,1)S(1)}, bf16[32,2,3,3,3]{0,1,4,3,2:T(2,128)(2,1)}, u32[]{:S(2)}) copy-start(bf16[32,2,3,3,3]{0,1,4,3,2:T(2,128)(2,1)} %param.15) | copy-start | bytes 10372
  61.9 9.2 %all-to-all-start = ((bf16[8,18,2,2,128]{4,3,2,1,0:T(2,128)(2,1)}), bf16[8,18,2,2,128]{4,3,2,1,0:T(2,128)(2,1)S(1)}, u32[]{:S(2)}, u32[]{:S(2)}) async-start(bf16[8,18,2,2,128]{4,3,2,1,0:T(2,128)(2,1)} %copy.22), calls=%async_computation | async-start | bytes 294912 | tf_op jit(solution)/shard_map/all_to_all | solution.py:434
  67.7 3.7 %copy-start = (bf16[3,32,32,3,3,3]{2,1,5,4,3,0:T(8,128)(2,1)S(1)}, bf16[3,32,32,3,3,3]{2,1,5,4,3,0:T(8,128)(2,1)}, u32[]{:S(2)}) copy-start(bf16[3,32,32,3,3,3]{2,1,5,4,3,0:T(8,128)(2,1)} %param.16) | copy-start | bytes 497668
  71.4 26.7 %copy-start.1 = (f32[2,2,64,128]{3,2,1,0:T(8,128)S(1)}, f32[2,2,64,128]{3,2,1,0:T(8,128)}, u32[]{:S(2)}) copy-start(f32[2,2,64,128]{3,2,1,0:T(8,128)} %get-tuple-element.18) | copy-start | bytes 393220
where the time goes:
time: 99.8 us; the launch traced here: 99.4 us
  Pallas kernels  77.3 us (77%)
  blocking collectives  7.92 us (8%)
  local copies, waits for them, and re-layouts  3.95 us (4%)
  starting transfers between devices  3.52 us (4%)
  waiting for transfers between devices  3.22 us (3%)
  other arithmetic  2.71 us (3%)
    pallas_call x1, Pallas kernels, gradients(): pl.pallas_call(functools.partial(gradients_kernel, shares, coils), out_sh...  58.6 us
    pallas_call x1, Pallas kernels, denoise(): pl.pallas_call(functools.partial(denoise_kernel, x_outs, y_outs, group, r...  18.7 us
    all_to_all x1, blocking collectives, body(): taken = lax.all_to_all(pieces, 'slab', 0, 0)  7.92 us
    all_to_all x1, starting transfers between devices, body(): taken = lax.all_to_all(pieces, 'slab', 0, 0)  3.52 us
    all_to_all x1, waiting for transfers between devices, body(): taken = lax.all_to_all(pieces, 'slab', 0, 0)  3.22 us
  transfers between devices with their start and end apart: 1, of which 1 were waited for; matrix products, arithmetic and copies ran while one was open for 2% of the time, Pallas kernels for 0%

commit v1 on v0

--- a/solution.py
+++ b/solution.py
@@ -22,7 +22,7 @@
     table = table.astype(np.float32)
     high = table.astype(jnp.bfloat16)
     low = (table - high.astype(np.float32)).astype(jnp.bfloat16)
-    return jnp.asarray(high), jnp.asarray(low)
+    return high, low
 
 
 def split(values):
@@ -34,17 +34,15 @@
     return jnp.dot(left, right, preferred_element_type=jnp.float32)
 
 
-def transform(real, imag, y_high, y_low, z_high, z_low):
+def transform(real, imag, y_table, z_table):
     rows, width = real.shape
     high, low = split(jnp.concatenate([real, imag], axis=1))
-    both = multiply(y_high[...], jnp.concatenate([high, low], axis=1))
-    field = both[:, : 2 * width] + both[:, 2 * width :] + multiply(y_low[...], high)
+    field = multiply(y_table[...], jnp.concatenate([high, low, high], axis=0))
     field = jnp.concatenate(
         [field[:rows, :width] + field[rows:, width:], field[:rows, width:] - field[rows:, :width]], axis=1
     )
     high, low = split(field)
-    both = multiply(jnp.concatenate([high, low], axis=0), z_high[...])
-    field = both[:rows] + both[rows:] + multiply(high, z_low[...])
+    field = multiply(jnp.concatenate([high, low, high], axis=1), z_table[...])
     return field[:, :width], field[:, width:]
 
 
@@ -52,9 +50,39 @@
     return jnp.sum(jnp.sum(values, axis=0, keepdims=True), axis=1, keepdims=True)
 
 
+BIAS = 128
+LOW_HALF = 65535
+
+
+def pack(real, imag):
+    largest = jnp.maximum(
+        jnp.max(jnp.abs(real), axis=0, keepdims=True), jnp.max(jnp.abs(imag), axis=0, keepdims=True)
+    )
+    exponent = jnp.maximum(jnp.ceil(jnp.log2(jnp.maximum(largest, 1e-35)) - 14.98), -110.0)
+    scale = jnp.exp2(-exponent)
+    real = jnp.round(real * scale).astype(jnp.int32)
+    imag = jnp.round(imag * scale).astype(jnp.int32)
+    code = exponent.astype(jnp.int32) + BIAS
+    places = lax.broadcasted_iota(jnp.int32, (8, real.shape[1]), 0)
+    bits = jnp.bitwise_and(jnp.right_shift(jnp.broadcast_to(code, places.shape), places), 1)
+    head = jnp.bitwise_or(jnp.bitwise_and(real[:8], -2), bits)
+    real = jnp.concatenate([head, real[8:]], axis=0)
+    return jnp.bitwise_or(jnp.left_shift(real, 16), jnp.bitwise_and(imag, LOW_HALF))
+
+
+def unpack(words):
+    real = jnp.right_shift(words, 16)
+    imag = jnp.right_shift(jnp.left_shift(words, 16), 16)
+    places = lax.broadcasted_iota(jnp.int32, (8, words.shape[1]), 0)
+    bits = jnp.left_shift(jnp.bitwise_and(real[:8], 1), places)
+    code = jnp.sum(bits, axis=0, keepdims=True)
+    scale = jnp.exp2((code - BIAS).astype(jnp.float32))
+    return real.astype(jnp.float32) * scale, imag.astype(jnp.float32) * scale
+
+
 def gradients_kernel(
-    shares, coils, maps, measured, mask, prior, y_high, y_low, z_high, z_low,
-    out, beside, part, arrived, rhs, spectrum, own_residual, residual, note, notes, edges,
+    shares, coils, maps, measured, mask, prior, y_table, z_table,
+    out, beside, part, outbox, inbox, own_rhs, rhs, own_residual, residual, note, notes, edges,
     block_send, block_recv, note_send, note_recv, edge_send, edge_recv,
 ):
     slab = lax.axis_index("slab")
@@ -63,7 +91,7 @@
     me = slab * coils + coil
     planes = maps.shape[1]
     block = prior.shape[2]
-    tables = (y_high, y_low, z_high, z_low)
+    tables = (y_table, z_table)
 
     def device_at(distance):
         other = lax.rem(me + distance, devices)
@@ -72,7 +100,6 @@
     barrier = pltpu.get_barrier_semaphore()
     for distance in range(1, devices):
         pl.semaphore_signal(barrier, inc=1, device_id=device_at(distance), device_id_type=MESH)
-    pl.semaphore_wait(barrier, devices - 1)
 
     def rows_of(index):
         return pl.ds(pl.multiple_of(index * block, block), block)
@@ -85,10 +112,10 @@
             target = lax.rem(coil + distance, coils)
             copies.append(
                 pltpu.make_async_remote_copy(
-                    src_ref=part.at[phase, :, p, rows_of(target)],
-                    dst_ref=arrived.at[phase, distance - 1, :, p],
-                    send_sem=block_send.at[2 * phase, p, distance - 1],
-                    recv_sem=block_recv.at[2 * phase, p, distance - 1],
+                    src_ref=outbox.at[phase, p, rows_of(target)],
+                    dst_ref=inbox.at[phase, distance - 1, p],
+                    send_sem=block_send.at[phase, p, distance - 1],
+                    recv_sem=block_recv.at[phase, p, distance - 1],
                     device_id=(slab, target),
                     device_id_type=MESH,
                 )
@@ -97,15 +124,32 @@
             copy.start()
         return copies
 
-    def gather(buffer, phase, p):
+    def gather_rhs(p):
         copies = []
         for distance in range(1, coils):
             copies.append(
                 pltpu.make_async_remote_copy(
-                    src_ref=buffer.at[:, p, mine],
-                    dst_ref=buffer.at[:, p, mine],
-                    send_sem=block_send.at[2 * phase + 1, p, distance - 1],
-                    recv_sem=block_recv.at[2 * phase + 1, p, distance - 1],
+                    src_ref=outbox.at[2, p, pl.ds(0, block)],
+                    dst_ref=inbox.at[2, distance - 1, p],
+                    send_sem=block_send.at[2, p, distance - 1],
+                    recv_sem=block_recv.at[2, p, distance - 1],
+                    device_id=(slab, lax.rem(coil + distance, coils)),
+                    device_id_type=MESH,
+                )
+            )
+        for copy in copies:
+            copy.start()
+        return copies
+
+    def gather(p):
+        copies = []
+        for distance in range(1, coils):
+            copies.append(
+                pltpu.make_async_remote_copy(
+                    src_ref=residual.at[:, p, mine],
+                    dst_ref=residual.at[:, p, mine],
+                    send_sem=block_send.at[3, p, distance - 1],
+                    recv_sem=block_recv.at[3, p, distance - 1],
                     device_id=(slab, lax.rem(coil + distance, coils)),
                     device_id_type=MESH,
                 )
@@ -131,19 +175,19 @@
             copy.start()
         return copies
 
-    margin = edges.shape[3]
+    margin = edges.shape[4]
     above = lax.rem(coil + coils - 1, coils)
     below = lax.rem(coil + 1, coils)
 
-    def send_edges(p):
+    def send_edges(source, which, p):
         copies = []
         for side, first, target in ((0, block - margin, below), (1, 0, above)):
             copies.append(
                 pltpu.make_async_remote_copy(
-                    src_ref=own_residual.at[:, p, first : first + margin],
-                    dst_ref=edges.at[side, :, p],
-                    send_sem=edge_send.at[side, p],
-                    recv_sem=edge_recv.at[side, p],
+                    src_ref=source.at[:, p, first : first + margin],
+                    dst_ref=edges.at[which, side, :, p],
+                    send_sem=edge_send.at[which, side, p],
+                    recv_sem=edge_recv.at[which, side, p],
                     device_id=(slab, target),
                     device_id_type=MESH,
                 )
@@ -172,8 +216,13 @@
 
     def backward_part(real, imag, phase, p):
         imag, real = transform(imag, real, *tables)
-        part[phase, 0, p] = maps[0, p] * real + maps[1, p] * imag
-        part[phase, 1, p] = maps[0, p] * imag - maps[1, p] * real
+        part_re = maps[0, p] * real + maps[1, p] * imag
+        part_im = maps[0, p] * imag - maps[1, p] * real
+        part[phase, 0, p] = part_re
+        part[phase, 1, p] = part_im
+        for index in range(coils):
+            span = slice(index * block, (index + 1) * block)
+            outbox[phase, p, span] = pack(part_re[span], part_im[span])
 
     def forward(image_re, image_im, p):
         real = maps[0, p] * image_re - maps[1, p] * image_im
@@ -182,38 +231,52 @@
         sampled = mask[p].astype(jnp.float32)
         return real * sampled, imag * sampled
 
-    def reduced(phase, h, p):
-        value = part[phase, h, p, mine]
+    def reduced(phase, p):
+        real = part[phase, 0, p, mine]
+        imag = part[phase, 1, p, mine]
         for distance in range(1, coils):
-            value = value + arrived[phase, distance - 1, h, p]
-        return value
-
-    pending = []
+            more = unpack(inbox[phase, distance - 1, p])
+            real = real + more[0]
+            imag = imag + more[1]
+        return real, imag
+
     for p in range(planes):
         sampled = mask[p].astype(jnp.float32)
         backward_part(measured[0, p] * sampled, measured[1, p] * sampled, 0, p)
-        pending.append(scatter(0, p))
+    pl.semaphore_wait(barrier, devices - 1)
+    pending = [scatter(0, p) for p in range(planes)]
     gathers = []
     norm = jnp.zeros((1, 1), jnp.float32)
+    edge_copies = []
     for p in range(planes):
         finish(pending[p])
-        for h in range(2):
-            value = reduced(0, h, p) + LAMBDA * prior[h, p]
-            rhs[h, p, mine] = value
-            norm = norm + total_of(value * value)
-        gathers.append(gather(rhs, 0, p))
+        real, imag = reduced(0, p)
+        real = real + LAMBDA * prior[0, p]
+        imag = imag + LAMBDA * prior[1, p]
+        outbox[2, p, :block] = pack(real, imag)
+        gathers.append(gather_rhs(p))
+        own_rhs[0, p] = real
+        own_rhs[1, p] = imag
+        rhs[0, p, mine] = real
+        rhs[1, p, mine] = imag
+        norm = norm + total_of(real * real) + total_of(imag * imag)
+    for p in range(planes):
+        edge_copies.extend(send_edges(own_rhs, 0, p))
     energy = LAMBDA * norm
     pending = []
     for p in range(planes):
         finish(gathers[p])
-        result = forward(rhs[0, p], rhs[1, p], p)
-        for h in range(2):
-            spectrum[h, p] = result[h]
-            energy = energy + total_of(result[h] * result[h])
+        for distance in range(1, coils):
+            source = rows_of(lax.rem(coil + coils - distance, coils))
+            real, imag = unpack(inbox[2, distance - 1, p])
+            rhs[0, p, source] = real
+            rhs[1, p, source] = imag
+        real, imag = forward(rhs[0, p], rhs[1, p], p)
+        energy = energy + total_of(real * real) + total_of(imag * imag)
         if p == planes - 1:
             write_note(0, [norm, energy])
             first_notes = tell(0)
-        backward_part(spectrum[0, p], spectrum[1, p], 1, p)
+        backward_part(real, imag, 1, p)
         pending.append(scatter(1, p))
     finish(first_notes)
     norm, curvature = read_notes(0, 2)
@@ -223,36 +286,40 @@
     cross = jnp.zeros((1, 1), jnp.float32)
     for p in range(planes):
         finish(pending[p])
+        images = reduced(1, p)
         for h in range(2):
-            direction = rhs[h, p, mine]
-            value = direction - step * (reduced(1, h, p) + LAMBDA * direction)
+            direction = own_rhs[h, p]
+            image = images[h] + LAMBDA * direction
+            value = direction - step * image
             own_residual[h, p] = value
             residual[h, p, mine] = value.astype(jnp.bfloat16)
+        gathers.append(gather(p))
+        for h in range(2):
+            value = own_residual[h, p]
+            image = images[h] + LAMBDA * own_rhs[h, p]
             norm_next = norm_next + total_of(value * value)
-            cross = cross + LAMBDA * total_of(value * direction)
-        gathers.append(gather(residual, 1, p) + send_edges(p))
+            cross = cross + total_of(value * image)
+    for p in range(planes):
+        edge_copies.extend(send_edges(own_residual, 1, p))
     energy = LAMBDA * norm_next
     for p in range(planes):
         finish(gathers[p])
-        result = forward(residual[0, p].astype(jnp.float32), residual[1, p].astype(jnp.float32), p)
-        for h in range(2):
-            energy = energy + total_of(result[h] * result[h])
-            cross = cross + total_of(result[h] * spectrum[h, p])
+        real, imag = forward(residual[0, p].astype(jnp.float32), residual[1, p].astype(jnp.float32), p)
+        energy = energy + total_of(real * real) + total_of(imag * imag)
     write_note(1, [norm_next, energy, cross])
     finish(tell(1))
     norm_next, energy, cross = read_notes(1, 3)
     ratio = norm_next / norm
     curvature = energy + 2.0 * ratio * cross + ratio * ratio * curvature
     step_next = norm_next / curvature
+    finish(edge_copies)
     for h in range(2):
         for p in range(planes):
-            direction = rhs[h, p, mine]
+            direction = own_rhs[h, p]
             out[h, p] = step * direction + step_next * (own_residual[h, p] + ratio * direction)
-            for side, start, inside in (
-                (0, above * block + block - margin, coil > 0), (1, below * block, coil < coils - 1)
-            ):
-                direction = rhs[h, p, pl.ds(pl.multiple_of(start, margin), margin)]
-                value = step * direction + step_next * (edges[side, h, p] + ratio * direction)
+            for side, inside in ((0, coil > 0), (1, coil < coils - 1)):
+                direction = edges[0, side, h, p]
+                value = step * direction + step_next * (edges[1, side, h, p] + ratio * direction)
                 beside[side, h, p] = jnp.where(inside, value, 0.0)
 
 
@@ -262,38 +329,41 @@
     shares = lax.axis_size("slab")
     coils = lax.axis_size("coil")
     cosine, sine = dft_parts(rows)
-    y_tables = halves(np.concatenate([cosine, sine]))
+    high, low = halves(np.concatenate([cosine, sine]))
+    y_table = np.concatenate([high, high, low], axis=1)
     cosine, sine = dft_parts(width)
-    z_tables = halves(np.block([[cosine, -sine], [sine, cosine]]))
+    high, low = halves(np.block([[cosine, -sine], [sine, cosine]]))
+    z_table = np.concatenate([high, high, low], axis=0)
     image = (2, planes, rows, width)
     brick = (2, planes, block, width)
     margins = (2, 2, planes, margin, width)
     return pl.pallas_call(
         functools.partial(gradients_kernel, shares, coils),
         out_shape=[jax.ShapeDtypeStruct(dims, jnp.float32) for dims in (brick, margins)],
-        in_specs=[pl.BlockSpec(memory_space=pltpu.VMEM)] * 8,
+        in_specs=[pl.BlockSpec(memory_space=pltpu.VMEM)] * 6,
         out_specs=[pl.BlockSpec(memory_space=pltpu.VMEM)] * 2,
         scratch_shapes=[
             pltpu.VMEM((2,) + image, jnp.float32),
-            pltpu.VMEM((2, coils - 1) + brick, jnp.float32),
-            pltpu.VMEM(image, jnp.float32),
+            pltpu.VMEM((3, planes, rows, width), jnp.int32),
+            pltpu.VMEM((3, coils - 1, planes, block, width), jnp.int32),
+            pltpu.VMEM(brick, jnp.float32),
             pltpu.VMEM(image, jnp.float32),
             pltpu.VMEM(brick, jnp.float32),
             pltpu.VMEM(image, jnp.bfloat16),
             pltpu.VMEM((2, 1, 128), jnp.float32),
             pltpu.VMEM((2, shares * coils - 1, 1, 128), jnp.float32),
-            pltpu.VMEM(margins, jnp.float32),
+            pltpu.VMEM((2,) + margins, jnp.float32),
             pltpu.SemaphoreType.DMA((4, planes, coils - 1)),
             pltpu.SemaphoreType.DMA((4, planes, coils - 1)),
             pltpu.SemaphoreType.DMA((2, shares * coils - 1)),
             pltpu.SemaphoreType.DMA((2, shares * coils - 1)),
-            pltpu.SemaphoreType.DMA((2, planes)),
-            pltpu.SemaphoreType.DMA((2, planes)),
+            pltpu.SemaphoreType.DMA((2, 2, planes)),
+            pltpu.SemaphoreType.DMA((2, 2, planes)),
         ],
         compiler_params=pltpu.CompilerParams(
             collective_id=0, has_side_effects=True, vmem_limit_bytes=56 * 1024 * 1024
         ),
-    )(maps, measured, mask, prior, *y_tables, *z_tables)
+    )(maps, measured, mask, prior, y_table, z_table)
 
 
 def block_weights(weight, x_outs, y_outs, in_pad, out_pad):

time: 99.8 us -> 85.4 us (0.86)
  Pallas kernels: 77.3 us -> 63 us
    pallas_call x1, Pallas kernels: 58.6 us -> 44.4 us  [gradients(): pl.pallas_call(functools.partial(gradients_kernel, shares, coils), out_sh...]
  transfers between devices with their start and end apart: 1 -> 1, of which waited for: 1 -> 1; matrix products, arithmetic and copies ran while one was open for 2% -> 3% of each run, Pallas kernels for 0% -> 0%
where the time goes in v1:
time: 85.4 us; the launch traced here: 85 us
  Pallas kernels  63 us (74%)
  blocking collectives  7.92 us (9%)
  local copies, waits for them, and re-layouts  3.95 us (5%)
  starting transfers between devices  3.38 us (4%)
  waiting for transfers between devices  3.15 us (4%)
  other arithmetic  2.71 us (3%)
  between operations  0.87 us (1%)
    pallas_call x1, Pallas kernels, gradients(): pl.pallas_call(functools.partial(gradients_kernel, shares, coils), out_sh...  44.4 us
    pallas_call x1, Pallas kernels, denoise(): pl.pallas_call(functools.partial(denoise_kernel, x_outs, y_outs, group, r...  18.7 us
    all_to_all x1, blocking collectives, body(): taken = lax.all_to_all(pieces, 'slab', 0, 0)  7.92 us
    all_to_all x1, starting transfers between devices, body(): taken = lax.all_to_all(pieces, 'slab', 0, 0)  3.38 us
    all_to_all x1, waiting for transfers between devices, body(): taken = lax.all_to_all(pieces, 'slab', 0, 0)  3.15 us
  transfers between devices with their start and end apart: 1, of which 1 were waited for; matrix products, arithmetic and copies ran while one was open for 3% of the time, Pallas kernels for 0%

profile of v1, /device:TPU:0, one launch (start us, length us, event | category | flops | bytes accessed | tf_op | source)
XLA Modules:
  0.0 85.0 jit_solution(11824252446558818493)
XLA Ops:
  0.6 44.4 %shard_map.104 = (f32[2,2,64,128]{3,2,1,0:T(8,128)}, f32[2,2,2,8,128]{4,3,2,1,0:T(8,128)}) custom-call(f32[2,2,256,128]{3,2,1,0:T(8,128)} %bitcast.78, f32[2,2,256,128]{3,2,1,0:T(8,128)} %bitcast.79, s32[2,256,128]{2,1,0:T(8,128)} %mask.1, f32[2,2,64,128]{3,2,1,0:T(8,128)} %prior.1, bf16[512,768]{1,0:T(8,128)(2,1)} %constant.7.clone.y_table, ...), custom_call_target="tpu_custom_call" | custom-call | tf_op jit(solution)/shard_map/pallas_call | solution.py:340
  45.0 0.0 copy-start.2
  45.0 0.0 copy-start.3
  45.0 0.8 convert.11
  45.8 0.9 %convert.12 = bf16[2,2,64,128]{3,2,1,0:T(8,128)(2,1)S(1)} convert(f32[2,2,64,128]{3,2,1,0:T(8,128)} %get-tuple-element.18) | non-fusion elementwise | flops 32768 | bytes 196608 | tf_op jit(solution)/shard_map/convert.1
  46.9 0.8 copy.20
  47.7 3.4 %all-to-all-start = ((bf16[8,18,2,2,128]{4,3,2,1,0:T(2,128)(2,1)}), bf16[8,18,2,2,128]{4,3,2,1,0:T(2,128)(2,1)S(1)}, u32[]{:S(2)}, u32[]{:S(2)}) async-start(bf16[8,18,2,2,128]{4,3,2,1,0:T(2,128)(2,1)} %copy.20), calls=%async_computation | async-start | bytes 294912 | tf_op jit(solution)/shard_map/all_to_all | solution.py:504
  51.0 0.0 copy-done.2
  51.1 0.0 copy-done.3
  51.1 0.1 pad_bitcast_fusion.8
  51.2 0.1 pad_maximum_fusion.1
  51.3 0.2 copy.23
  51.5 0.3 reshape.25.final
  51.8 0.1 pad_bitcast_fusion.3
  51.9 0.2 pad_maximum_fusion
  52.2 0.5 copy.22
  52.7 0.7 reshape.23
  53.4 0.0 copy-start
  53.4 0.1 copy.24.first
  53.5 3.1 %all-to-all-done = bf16[8,18,2,2,128]{4,3,2,1,0:T(2,128)(2,1)S(1)} async-done(((bf16[8,18,2,2,128]{4,3,2,1,0:T(2,128)(2,1)}), bf16[8,18,2,2,128]{4,3,2,1,0:T(2,128)(2,1)S(1)}, u32[]{:S(2)}, u32[]{:S(2)}) %all-to-all-start) | async-done | bytes 147488 | tf_op jit(solution)/shard_map/all_to_all | solution.py:504
  56.7 0.1 copy.21
  56.8 0.2 pad.44.features
  57.0 0.0 copy-done
  57.0 0.0 copy-start.1
  57.0 18.7 %shard_map.105 = f32[8,16,8,128]{3,2,1,0:T(8,128)S(1)} custom-call(bf16[18,18,16,128]{3,2,1,0:T(8,128)(2,1)S(1)} %pad.44.features, bf16[384,256]{1,0:T(8,128)(2,1)S(1)} %copy.24.first, bf16[3,3,3,96,32]{4,3,2,1,0:T(8,128)(2,1)S(1)} %bitcast.75, bf16[96,512]{1,0:T(8,128)(2,1)S(1)} %reshape.25.final), custom_call_target="tpu_custom_call" | custom-call | tf_op jit(solution)/shard_map/pallas_call | solution.py:481
  75.8 7.9 %all_to_all.10 = f32[8,8,2,2,128]{4,3,2,1,0:T(2,128)S(1)} all-to-all(f32[8,8,2,2,128]{4,3,2,1,0:T(2,128)S(1)} %bitcast.81), channel_id=1, replica_groups=mesh['slab'=8,'coil'=4] {'slab'}, dimensions={0} | all-to-all | bytes 262144 | tf_op jit(solution)/shard_map/all_to_all | solution.py:509
  83.7 0.0 copy-done.1
  83.7 0.7 bitcast_add_fusion
  84.4 0.7 copy.38
  (14 shorter events, 0.2 us)
Async XLA Ops:
  45.0 6.0 %copy-start.2 = (bf16[2,32,3,3,3]{1,0,4,3,2:T(2,128)(2,1)S(1)}, bf16[2,32,3,3,3]{1,0,4,3,2:T(2,128)(2,1)}, u32[]{:S(2)}) copy-start(bf16[2,32,3,3,3]{1,0,4,3,2:T(2,128)(2,1)} %param.15) | copy-start | bytes 10372
  45.0 6.1 %copy-start.3 = (bf16[32,2,3,3,3]{0,1,4,3,2:T(2,128)(2,1)S(1)}, bf16[32,2,3,3,3]{0,1,4,3,2:T(2,128)(2,1)}, u32[]{:S(2)}) copy-start(bf16[32,2,3,3,3]{0,1,4,3,2:T(2,128)(2,1)} %param.13) | copy-start | bytes 10372
  47.7 9.0 %all-to-all-start = ((bf16[8,18,2,2,128]{4,3,2,1,0:T(2,128)(2,1)}), bf16[8,18,2,2,128]{4,3,2,1,0:T(2,128)(2,1)S(1)}, u32[]{:S(2)}, u32[]{:S(2)}) async-start(bf16[8,18,2,2,128]{4,3,2,1,0:T(2,128)(2,1)} %copy.20), calls=%async_computation | async-start | bytes 294912 | tf_op jit(solution)/shard_map/all_to_all | solution.py:504
  53.4 3.6 %copy-start = (bf16[3,32,32,3,3,3]{2,1,5,4,3,0:T(8,128)(2,1)S(1)}, bf16[3,32,32,3,3,3]{2,1,5,4,3,0:T(8,128)(2,1)}, u32[]{:S(2)}) copy-start(bf16[3,32,32,3,3,3]{2,1,5,4,3,0:T(8,128)(2,1)} %param.14) | copy-start | bytes 497668
  57.0 26.7 %copy-start.1 = (f32[2,2,64,128]{3,2,1,0:T(8,128)S(1)}, f32[2,2,64,128]{3,2,1,0:T(8,128)}, u32[]{:S(2)}) copy-start(f32[2,2,64,128]{3,2,1,0:T(8,128)} %get-tuple-element.18) | copy-start | bytes 393220

commit v2 on v1

v2 whole, which is shorter than its diff:
```python
import functools

import jax
import jax.numpy as jnp
import numpy as np
from jax import lax
from jax.experimental import pallas as pl
from jax.experimental.pallas import tpu as pltpu
from jax.sharding import PartitionSpec as P

LAMBDA = 0.5
MESH = pl.DeviceIdType.MESH


def dft_parts(length):
    positions = np.arange(length)
    angles = 2.0 * np.pi / length * (positions[:, None] * positions[None, :] % length)
    return np.cos(angles) / np.sqrt(length), np.sin(angles) / np.sqrt(length)


def halves(table):
    table = table.astype(np.float32)
    high = table.astype(jnp.bfloat16)
    low = (table - high.astype(np.float32)).astype(jnp.bfloat16)
    return high, low


def split(values):
    high = values.astype(jnp.bfloat16)
    return high, (values - high.astype(jnp.float32)).astype(jnp.bfloat16)


def multiply(left, right):
    return jnp.dot(left, right, preferred_element_type=jnp.float32)


def transform(real, imag, y_table, z_table):
    rows, width = real.shape
    high, low = split(jnp.concatenate([real, imag], axis=1))
    field = multiply(y_table[...], jnp.concatenate([high, low, high], axis=0))
    field = jnp.concatenate(
        [field[:rows, :width] + field[rows:, width:], field[:rows, width:] - field[rows:, :width]], axis=1
    )
    high, low = split(field)
    field = multiply(jnp.concatenate([high, low, high], axis=1), z_table[...])
    return field[:, :width], field[:, width:]


def total_of(values):
    return jnp.sum(jnp.sum(values, axis=0, keepdims=True), axis=1, keepdims=True)


BIAS = 128
LOW_HALF = 65535


def pack(real, imag):
    largest = jnp.maximum(
        jnp.max(jnp.abs(real), axis=0, keepdims=True), jnp.max(jnp.abs(imag), axis=0, keepdims=True)
    )
    exponent = jnp.maximum(jnp.ceil(jnp.log2(jnp.maximum(largest, 1e-35)) - 14.98), -110.0)
    scale = jnp.exp2(-exponent)
    real = jnp.round(real * scale).astype(jnp.int32)
    imag = jnp.round(imag * scale).astype(jnp.int32)
    code = exponent.astype(jnp.int32) + BIAS
    places = lax.broadcasted_iota(jnp.int32, (8, real.shape[1]), 0)
    bits = jnp.bitwise_and(jnp.right_shift(jnp.broadcast_to(code, places.shape), places), 1)
    head = jnp.bitwise_or(jnp.bitwise_and(real[:8], -2), bits)
    real = jnp.concatenate([head, real[8:]], axis=0)
    return jnp.bitwise_or(jnp.left_shift(real, 16), jnp.bitwise_and(imag, LOW_HALF))


def unpack(words):
    real = jnp.right_shift(words, 16)
    imag = jnp.right_shift(jnp.left_shift(words, 16), 16)
    places = lax.broadcasted_iota(jnp.int32, (8, words.shape[1]), 0)
    bits = jnp.left_shift(jnp.bitwise_and(real[:8], 1), places)
    code = jnp.sum(bits, axis=0, keepdims=True)
    scale = jnp.exp2((code - BIAS).astype(jnp.float32))
    return real.astype(jnp.float32) * scale, imag.astype(jnp.float32) * scale


def spread(blocks, x_out):
    empty = jnp.zeros_like(blocks[0])
    return jnp.concatenate([empty] * x_out + blocks + [empty] * (1 - x_out), axis=1)


def first_weights(taps, base, table):
    outs = taps.shape[-1]
    for u in range(3):
        for v in range(3):
            for t in range(3):
                index = ((v * 3 + t) * 3 + u) * 2
                base[index : index + 2, :outs] = taps[u, v, t].astype(jnp.float32)
    window = (24, table.shape[0])
    row = lax.broadcasted_iota(jnp.int32, window, 0)
    place = row - 2 * (lax.broadcasted_iota(jnp.int32, window, 1) // outs) - 2
    rest = jnp.zeros((8, window[1]), jnp.float32)
    blocks = []
    for v in range(3):
        for t in range(3):
            block = jnp.zeros(window, jnp.float32)
            for k in range(6):
                index = (v * 3 + t) * 6 + k
                line = jnp.concatenate([base[index : index + 1, :outs]] * (window[1] // outs), axis=1)
                block = jnp.where(place == k, line, block)
            blocks.append(block)
        blocks.append(rest)
    blocks.append(jnp.zeros((16, window[1]), jnp.float32))
    table[...] = jnp.transpose(jnp.concatenate(blocks, axis=0)).astype(table.dtype)


def middle_weights(taps, table, y_outs):
    count, channels = taps.shape[3:]
    span = 4 * channels
    table[...] = jnp.zeros(table.shape, table.dtype)
    for layer in range(taps.shape[0]):
        for v in range(3):
            for x_out in range(2):
                block = spread([taps[layer, u, v] for u in range(3)], x_out)
                for y_out in range(y_outs):
                    base = (x_out * y_outs + y_out) * count
                    y_in = y_out + v
                    table[layer, base : base + count, y_in * span : (y_in + 1) * span] = block


def last_weights(taps, table, tall):
    channels = taps.shape[-1]
    span = 4 * channels
    row = lax.broadcasted_iota(jnp.int32, (tall, span), 0)
    for t in range(3):
        for x_out in range(2):
            lines = [spread([taps[u, v, t].astype(jnp.float32) for u in range(3)], x_out) for v in range(3)]
            for o in range(2):
                base = ((t * 2 + x_out) * 2 + o) * tall
                for y_in in range(table.shape[1] // span):
                    block = jnp.zeros((tall, span), jnp.float32)
                    for v in range(3):
                        block = jnp.where(row == y_in - v, lines[v][o : o + 1], block)
                    table[base : base + tall, y_in * span : (y_in + 1) * span] = block.astype(table.dtype)


def along_z(before, centre, after, lanes):
    width = centre.shape[1]
    before = jnp.where(lanes == 0, 0.0, pltpu.roll(before, 1, 1))
    after = jnp.where(lanes == width - 1, 0.0, pltpu.roll(after, width - 1, 1))
    return centre + before + after


def conv_first(table, taken, sink, rows, top, height):
    outs = sink.shape[2]
    width = sink.shape[3]
    depth = 3 * taken.shape[1]
    for y in range(rows):
        inside = jnp.logical_and(top + y >= 0, top + y < height)
        product = multiply(table[:, :depth], taken[y : y + 3].reshape(depth, taken.shape[2]))
        for group in range(taken.shape[2] // width):
            for q in range(table.shape[0] // outs):
                value = product[q * outs : (q + 1) * outs, group * width : (group + 1) * width]
                value = jnp.where(inside, jnp.maximum(value, 0.0), 0.0)
                sink[y, group * (table.shape[0] // outs) + q + 1] = value.astype(jnp.bfloat16)


def conv_middle(table, source, sink, rows, y_outs, top, height):
    planes, outs, width = source.shape[1] - 2, source.shape[2], source.shape[3]
    lanes = lax.broadcasted_iota(jnp.int32, (outs, width), 1)
    depth = (y_outs + 2) * 4 * outs
    group = 2 if planes % 4 == 0 else 1
    for y in range(0, rows, y_outs):
        for first in range(0, planes, 2 * group):
            taken = [
                source[y : y + y_outs + 2, first + 2 * k : first + 2 * k + 4].reshape(depth, width)
                for k in range(group)
            ]
            product = multiply(table[...], jnp.concatenate(taken, axis=1))
            for x_out in range(2):
                for y_out in range(y_outs):
                    base = (x_out * y_outs + y_out) * 3 * outs
                    inside = jnp.logical_and(top + y + y_out >= 0, top + y + y_out < height)
                    for k in range(group):
                        parts = [
                            product[base + t * outs : base + (t + 1) * outs, k * width : (k + 1) * width]
                            for t in range(3)
                        ]
                        value = along_z(*parts, lanes)
                        value = jnp.where(inside, jnp.maximum(value, 0.0), 0.0)
                        sink[y + y_out, first + 2 * k + x_out + 1] = value.astype(jnp.bfloat16)


def conv_last(table, source, sink, rows):
    planes, channels, width = source.shape[1] - 2, source.shape[2], source.shape[3]
    tall = table.shape[0] // 3
    lanes = lax.broadcasted_iota(jnp.int32, (tall, width), 1)
    depth = (rows + 2) * 4 * channels
    group = 2 if planes % 4 == 0 else 1
    for first in range(0, planes, 2 * group):
        taken = [
            source[: rows + 2, first + 2 * k : first + 2 * k + 4].reshape(depth, width) for k in range(group)
        ]
        product = multiply(table[...], jnp.concatenate(taken, axis=1))
        for k in range(group):
            parts = [product[t * tall : (t + 1) * tall, k * width : (k + 1) * width] for t in range(3)]
            sink[first // 2 + k] = along_z(*parts, lanes).reshape(sink.shape[1:])


def step_kernel(
    shares, coils, maps, measured, mask, prior, y_table, z_table, w_first, w_middle, w_last,
    out, refined,
    part, outbox, inbox, own_rhs, rhs, own_residual, residual, note, notes, fields, taken_fields,
    base, first_table, middle_table, last_table, shifted, even, odd, corrections, arrived,
    block_send, block_recv, note_send, note_recv, edge_send, edge_recv, field_send, field_recv, back_send, back_recv,
):
    slab = lax.axis_index("slab")
    coil = lax.axis_index("coil")
    devices = shares * coils
    me = slab * coils + coil
    planes = maps.shape[1]
    height, width = maps.shape[2:]
    block = prior.shape[2]
    rows = block // shares
    layers = w_middle.shape[0] + 2
    halo = layers
    y_outs = 2 if rows % 2 == 0 else 1
    tables = (y_table, z_table)

    def device_at(distance):
        other = lax.rem(me + distance, devices)
        return (other // coils, lax.rem(other, coils))

    barrier = pltpu.get_barrier_semaphore()
    for distance in range(1, devices):
        pl.semaphore_signal(barrier, inc=1, device_id=device_at(distance), device_id_type=MESH)

    def rows_of(index):
        return pl.ds(pl.multiple_of(index * block, block), block)

    mine = rows_of(coil)

    def send(source, target, send_sem, recv_sem, device):
        copy = pltpu.make_async_remote_copy(
            src_ref=source, dst_ref=target, send_sem=send_sem, recv_sem=recv_sem,
            device_id=device, device_id_type=MESH,
        )
        copy.start()
        return copy

    def to_coils(phase, p, source, target):
        copies = []
        for distance in range(1, coils):
            other = lax.rem(coil + distance, coils)
            copies.append(
                send(
                    source(other), target(distance), block_send.at[phase, p, distance - 1],
                    block_recv.at[phase, p, distance - 1], (slab, other),
                )
            )
        return copies

    def scatter(phase, p):
        return to_coils(
            phase, p, lambda other: outbox.at[phase, p, rows_of(other)],
            lambda distance: inbox.at[phase, distance - 1, p],
        )

    def gather_rhs(p):
        return to_coils(
            2, p, lambda other: outbox.at[2, p, pl.ds(0, block)], lambda distance: inbox.at[2, distance - 1, p]
        )

    def gather(p):
        return to_coils(
            3, p, lambda other: residual.at[:, p, mine], lambda distance: residual.at[:, p, mine]
        )

    def tell(phase):
        copies = []
        for distance in range(1, devices):
            copies.append(
                send(
                    note.at[phase], notes.at[phase, distance - 1], note_send.at[phase, distance - 1],
                    note_recv.at[phase, distance - 1], device_at(distance),
                )
            )
        return copies

    def send_edges(which):
        above = lax.rem(coil + coils - 1, coils)
        below = lax.rem(coil + 1, coils)
        ends = ((block, 0, below), (halo, halo + block, above))
        return [
            send(
                fields.at[which, pl.ds(source, halo)], fields.at[which, pl.ds(target, halo)],
                edge_send.at[which, side], edge_recv.at[which, side], (slab, other),
            )
            for side, (source, target, other) in enumerate(ends)
        ]

    deep = rows + 2 * halo

    def send_fields(which, copies):
        finish(copies)
        top_edge = fields[which, :halo]
        fields[which, :halo] = jnp.where(coil > 0, top_edge, 0.0)
        low_edge = fields[which, halo + block :]
        fields[which, halo + block :] = jnp.where(coil < coils - 1, low_edge, 0.0)
        copies = []
        for distance in range(1, shares):
            other = lax.rem(slab + distance, shares)
            copies.append(
                send(
                    fields.at[which, pl.ds(other * rows, deep)], taken_fields.at[which, :, slab + 1],
                    field_send.at[which, distance - 1], field_recv.at[which, distance - 1], (other, coil),
                )
            )
        taken_fields[which, :, slab + 1] = fields[which, pl.ds(slab * rows, deep)]
        return copies

    def finish(copies):
        for copy in copies:
            copy.wait()

    lanes = lax.broadcasted_iota(jnp.int32, (1, note.shape[2]), 1)

    def write_note(phase, values):
        line = jnp.zeros(lanes.shape, jnp.float32)
        for index, value in enumerate(values):
            line = jnp.where(lanes == index, value, line)
        note[phase] = line

    def read_notes(phase, count):
        line = note[phase]
        for distance in range(1, devices):
            line = line + notes[phase, distance - 1]
        return [jnp.sum(jnp.where(lanes == index, line, 0.0), axis=1, keepdims=True) for index in range(count)]

    def backward_part(real, imag, phase, p):
        imag, real = transform(imag, real, *tables)
        part_re = maps[0, p] * real + maps[1, p] * imag
        part_im = maps[0, p] * imag - maps[1, p] * real
        part[phase, 0, p] = part_re
        part[phase, 1, p] = part_im
        for index in range(coils):
            span = slice(index * block, (index + 1) * block)
            outbox[phase, p, span] = pack(part_re[span], part_im[span])

    def forward(image_re, image_im, p):
        real = maps[0, p] * image_re - maps[1, p] * image_im
        imag = maps[0, p] * image_im + maps[1, p] * image_re
        real, imag = transform(real, imag, *tables)
        sampled = mask[p].astype(jnp.float32)
        return real * sampled, imag * sampled

    def reduced(phase, p):
        real = part[phase, 0, p, mine]
        imag = part[phase, 1, p, mine]
        for distance in range(1, coils):
            more = unpack(inbox[phase, distance - 1, p])
            real = real + more[0]
            imag = imag + more[1]
        return real, imag

    pending = []
    for p in range(planes):
        sampled = mask[p].astype(jnp.float32)
        backward_part(measured[0, p] * sampled, measured[1, p] * sampled, 0, p)
        if p == 0:
            pl.semaphore_wait(barrier, devices - 1)
        pending.append(scatter(0, p))
    first_weights(w_first, base, first_table)
    last_weights(w_last, last_table, last_table.shape[0] // 12)
    total = taken_fields.shape[2]
    for which in range(2):
        for outer in (0, total - 1):
            taken_fields[which, :, outer] = jnp.zeros((deep,) + taken_fields.shape[3:], jnp.float32)
    shifted[...] = jnp.zeros(shifted.shape, shifted.dtype)
    for buffer in (even, odd):
        for outer in (0, buffer.shape[1] - 1):
            buffer[:, outer] = jnp.zeros((buffer.shape[0],) + buffer.shape[2:], buffer.dtype)
    gathers = []
    norm = jnp.zeros((1, 1), jnp.float32)
    for p in range(planes):
        finish(pending[p])
        real, imag = reduced(0, p)
        real = real + LAMBDA * prior[0, p]
        imag = imag + LAMBDA * prior[1, p]
        outbox[2, p, :block] = pack(real, imag)
        gathers.append(gather_rhs(p))
        for h, value in enumerate((real, imag)):
            own_rhs[h, p] = value
            rhs[h, p, mine] = value
            fields[0, halo : halo + block, 2 * p + h] = value
            norm = norm + total_of(value * value)
    edge_copies = send_edges(0)
    middle_weights(w_middle, middle_table, y_outs)
    energy = LAMBDA * norm
    pending = []
    for p in range(planes):
        finish(gathers[p])
        for distance in range(1, coils):
            source = rows_of(lax.rem(coil + coils - distance, coils))
            real, imag = unpack(inbox[2, distance - 1, p])
            rhs[0, p, source] = real
            rhs[1, p, source] = imag
        real, imag = forward(rhs[0, p], rhs[1, p], p)
        energy = energy + total_of(real * real) + total_of(imag * imag)
        if p == planes - 1:
            write_note(0, [norm, energy])
            first_notes = tell(0)
        backward_part(real, imag, 1, p)
        pending.append(scatter(1, p))
    field_copies = send_fields(0, edge_copies)
    finish(first_notes)
    norm, curvature = read_notes(0, 2)
    step = norm / curvature
    gathers = []
    norm_next = jnp.zeros((1, 1), jnp.float32)
    cross = jnp.zeros((1, 1), jnp.float32)
    for p in range(planes):
        finish(pending[p])
        images = reduced(1, p)
        for h in range(2):
            direction = own_rhs[h, p]
            image = images[h] + LAMBDA * direction
            value = direction - step * image
            own_residual[h, p] = value
            residual[h, p, mine] = value.astype(jnp.bfloat16)
            fields[1, halo : halo + block, 2 * p + h] = value
        gathers.append(gather(p))
        for h in range(2):
            value = own_residual[h, p]
            image = images[h] + LAMBDA * own_rhs[h, p]
            norm_next = norm_next + total_of(value * value)
            cross = cross + total_of(value * image)
    edge_copies = send_edges(1)
    energy = LAMBDA * norm_next
    for p in range(planes):
        finish(gathers[p])
        if p == planes - 1:
            field_copies = field_copies + send_fields(1, edge_copies)
        real, imag = forward(residual[0, p].astype(jnp.float32), residual[1, p].astype(jnp.float32), p)
        energy = energy + total_of(real * real) + total_of(imag * imag)
    write_note(1, [norm_next, energy, cross])
    last_notes = tell(1)
    finish(field_copies)
    finish(last_notes)
    norm_next, energy, cross = read_notes(1, 3)
    ratio = norm_next / norm
    curvature = energy + 2.0 * ratio * cross + ratio * ratio * curvature
    step_next = norm_next / curvature
    share = step + step_next * ratio
    across = lax.broadcasted_iota(jnp.int32, (4 * total, width), 1)
    for y in range(deep):
        line = share * taken_fields[0, y].reshape(4 * total, width)
        line = line + step_next * taken_fields[1, y].reshape(4 * total, width)
        line = line.astype(jnp.bfloat16).astype(jnp.float32)
        before = jnp.where(across == 0, 0.0, pltpu.roll(line, 1, 1))
        after = jnp.where(across == width - 1, 0.0, pltpu.roll(line, width - 1, 1))
        for group in range(shifted.shape[2] // width):
            span = slice(16 * group, 16 * group + 24)
            piece = jnp.concatenate([before[span], line[span], after[span], jnp.zeros((8, width), jnp.float32)], axis=0)
            shifted[y, :, group * width : (group + 1) * width] = piece.astype(jnp.bfloat16)
    for h in range(2):
        for p in range(planes):
            out[h, p] = share * own_rhs[h, p] + step_next * own_residual[h, p]
    top = coil * block + slab * rows
    left = layers - 1
    conv_first(first_table, shifted, even, rows + 2 * left, top - left, height)
    buffers = (even, odd)
    for layer in range(layers - 2):
        left = left - 1
        conv_middle(
            middle_table.at[layer], buffers[layer % 2], buffers[(layer + 1) % 2], rows + 2 * left, y_outs,
            top - left, height,
        )
    conv_last(last_table, buffers[(layers - 2) % 2], corrections, rows)
    copies = []
    for distance in range(1, shares):
        other = lax.rem(slab + distance, shares)
        copies.append(
            send(
                corrections.at[other], arrived.at[slab], back_send.at[distance - 1],
                back_recv.at[distance - 1], (other, coil),
            )
        )
    arrived[slab] = corrections[slab]
    finish(copies)
    for s in range(shares):
        span = slice(s * rows, (s + 1) * rows)
        for p in range(planes):
            for h in range(2):
                refined[h, p, span] = out[h, p, span] + arrived[s, 2 * p + h, :rows]


def body(sensitivity, kspace, sampling, prior_image, w_first, w_middle, w_last):
    maps, measured = sensitivity[0], kspace[0]
    planes, height, width = sampling.shape
    block = prior_image.shape[2]
    shares = lax.axis_size("slab")
    coils = lax.axis_size("coil")
    rows = block // shares
    channels = w_first.shape[0]
    layers = w_middle.shape[0] + 2
    whole = shares * planes
    y_outs = 2 if rows % 2 == 0 else 1
    cosine, sine = dft_parts(height)
    high, low = halves(np.concatenate([cosine, sine]))
    y_table = np.concatenate([high, high, low], axis=1)
    cosine, sine = dft_parts(width)
    high, low = halves(np.block([[cosine, -sine], [sine, cosine]]))
    z_table = np.concatenate([high, high, low], axis=0)
    w_first = jnp.transpose(w_first, (2, 3, 4, 1, 0))
    w_middle = jnp.transpose(w_middle, (0, 3, 4, 5, 1, 2)).reshape(layers - 2, 3, 3, 3 * channels, channels)
    w_last = jnp.transpose(w_last, (2, 3, 4, 0, 1))
    image = (2, planes, height, width)
    brick = (2, planes, block, width)
    tall = rows + -rows % 8
    deep = rows + 2 * layers
    hidden = (rows + 2 * (layers - 1), whole + 2, channels, width)
    kernel = pl.pallas_call(
        functools.partial(step_kernel, shares, coils),
        out_shape=[jax.ShapeDtypeStruct(brick, jnp.float32)] * 2,
        in_specs=[pl.BlockSpec(memory_space=pltpu.VMEM)] * 9,
        out_specs=[pl.BlockSpec(memory_space=pltpu.VMEM)] * 2,
        scratch_shapes=[
            pltpu.VMEM((2,) + image, jnp.float32),
            pltpu.VMEM((3, planes, height, width), jnp.int32),
            pltpu.VMEM((3, coils - 1, planes, block, width), jnp.int32),
            pltpu.VMEM(brick, jnp.float32),
            pltpu.VMEM(image, jnp.float32),
            pltpu.VMEM(brick, jnp.float32),
            pltpu.VMEM(image, jnp.bfloat16),
            pltpu.VMEM((2, 1, 128), jnp.float32),
            pltpu.VMEM((2, shares * coils - 1, 1, 128), jnp.float32),
            pltpu.VMEM((2, block + 2 * layers, 2 * planes, width), jnp.float32),
            pltpu.VMEM((2, deep, shares + 2, 2 * planes, width), jnp.float32),
            pltpu.VMEM((56, 128), jnp.float32),
            pltpu.VMEM((8 * channels, 256), jnp.bfloat16),
            pltpu.VMEM((layers - 2, 2 * y_outs * 3 * channels, (y_outs + 2) * 4 * channels), jnp.bfloat16),
            pltpu.VMEM((12 * tall, (rows + 2) * 4 * channels), jnp.bfloat16),
            pltpu.VMEM((deep, 80, whole // 8 * width), jnp.bfloat16),
            pltpu.VMEM(hidden, jnp.bfloat16),
            pltpu.VMEM(hidden, jnp.bfloat16),
            pltpu.VMEM((shares, 2 * planes, tall, width), jnp.float32),
            pltpu.VMEM((shares, 2 * planes, tall, width), jnp.float32),
            pltpu.SemaphoreType.DMA((4, planes, coils - 1)),
            pltpu.SemaphoreType.DMA((4, planes, coils - 1)),
            pltpu.SemaphoreType.DMA((2, shares * coils - 1)),
            pltpu.SemaphoreType.DMA((2, shares * coils - 1)),
            pltpu.SemaphoreType.DMA((2, 2)),
            pltpu.SemaphoreType.DMA((2, 2)),
            pltpu.SemaphoreType.DMA((2, shares - 1)),
            pltpu.SemaphoreType.DMA((2, shares - 1)),
            pltpu.SemaphoreType.DMA((shares - 1,)),
            pltpu.SemaphoreType.DMA((shares - 1,)),
        ],
        compiler_params=pltpu.CompilerParams(
            collective_id=0, has_side_effects=True, vmem_limit_bytes=56 * 1024 * 1024
        ),
    )
    return tuple(kernel(maps, measured, sampling, prior_image, y_table, z_table, w_first, w_middle, w_last))


def solution(mesh):
    placed = (
        P("coil", None, "slab", None, None),
        P("coil", None, "slab", None, None),
        P("slab", None, None),
        P(None, "slab", "coil", None),
        P(),
        P(),
        P(),
    )
    return jax.shard_map(
        body,
        mesh=mesh,
        in_specs=placed,
        out_specs=(P(None, "slab", "coil", None), P(None, "slab", "coil", None)),
        check_vma=False,
    )
```

time: 85.4 us -> 59.6 us (0.70)
  blocking collectives: 7.92 us -> 0 us
  Pallas kernels: 63 us -> 56.5 us
  starting transfers between devices: 3.38 us -> 0 us
  waiting for transfers between devices: 3.15 us -> 0 us
  other arithmetic: 2.71 us -> 0 us
  local copies, waits for them, and re-layouts: 3.95 us -> 2.26 us
    all_to_all x1 -> x0, blocking collectives: 7.92 us -> none  [body(): taken = lax.all_to_all(pieces, 'slab', 0, 0)]
    pallas_call x2 -> x1, Pallas kernels: 63 us -> 56.5 us  [body(): kernel(maps, measured, sampling, prior_image, y_table, z_table, w_first,...]
    all_to_all x1 -> x0, starting transfers between devices: 3.38 us -> none  [body(): taken = lax.all_to_all(pieces, 'slab', 0, 0)]
    all_to_all x1 -> x0, waiting for transfers between devices: 3.15 us -> none  [body(): taken = lax.all_to_all(pieces, 'slab', 0, 0)]
    another operation x4 -> x0, other arithmetic: 2.01 us -> none
    another operation x6 -> x0, local copies, waits for them, and re-layouts: 1.64 us -> none  [the longest x4 0.87 us: block_weights(): stacked = jnp.stack(parts)]
    unnamed x16 -> x4, local copies, waits for them, and re-layouts: 0.75 us -> 2.26 us
    reshape x4 -> x0, local copies, waits for them, and re-layouts: 1.17 us -> none  [the longest x3 1.15 us: block_weights(): stacked.reshape(stacked.shape[0] * stacked.shape[1] * stacked.shape[2], -1)]
  transfers between devices with their start and end apart: 1 -> 0, of which waited for: 1 -> 0; matrix products, arithmetic and copies ran while one was open for 3% -> 0% of each run, Pallas kernels for 0% -> 0%
where the time goes in v2:
time: 59.6 us; the launch traced here: 59.5 us
  Pallas kernels  56.5 us (95%)
  local copies, waits for them, and re-layouts  2.26 us (4%)
  between operations  0.65 us (1%)
    pallas_call x1, Pallas kernels, body(): kernel(maps, measured, sampling, prior_image, y_table, z_table, w_first,...  56.5 us
    unnamed x4, local copies, waits for them, and re-layouts  2.26 us

profile of v2, /device:TPU:0, one launch (start us, length us, event | category | flops | bytes accessed | tf_op | source)
XLA Modules:
  0.0 59.5 jit_solution(7100917084168443068)
XLA Ops:
  0.6 56.5 %shard_map.104 = (f32[2,2,64,128]{3,2,1,0:T(8,128)}, f32[2,2,64,128]{3,2,1,0:T(8,128)}) custom-call(f32[2,2,256,128]{3,2,1,0:T(8,128)} %bitcast.8, f32[2,2,256,128]{3,2,1,0:T(8,128)} %bitcast.9, s32[2,256,128]{2,1,0:T(8,128)} %mask.1, f32[2,2,64,128]{3,2,1,0:T(8,128)} %prior.1, bf16[512,768]{1,0:T(8,128)(2,1)} %constant.4.clone.y_table, ...), custom_call_target="tpu_custom_call" | custom-call | tf_op jit(solution)/shard_map/pallas_call | solution.py:560
  57.2 0.0 copy-start
  57.2 1.6 %copy.13 = f32[2,2,64,128]{3,2,1,0:T(8,128)} copy(f32[2,2,64,128]{3,2,1,0:T(8,128)} %get-tuple-element.4) | data formatting | bytes 262144
  58.8 0.0 copy-done
  58.8 0.7 %copy.14 = f32[2,2,64,128]{3,2,1,0:T(8,128)} copy(f32[2,2,64,128]{3,2,1,0:T(8,128)S(1)} %copy-done) | data formatting | bytes 262144
Async XLA Ops:
  57.2 1.6 %copy-start = (f32[2,2,64,128]{3,2,1,0:T(8,128)S(1)}, f32[2,2,64,128]{3,2,1,0:T(8,128)}, u32[]{:S(2)}) copy-start(f32[2,2,64,128]{3,2,1,0:T(8,128)} %get-tuple-element.5) | copy-start | bytes 393220

commit v3 on v2

--- a/solution.py
+++ b/solution.py
@@ -187,29 +187,39 @@
                         sink[y + y_out, first + 2 * k + x_out + 1] = value.astype(jnp.bfloat16)
 
 
-def conv_last(table, source, sink, rows):
-    planes, channels, width = source.shape[1] - 2, source.shape[2], source.shape[3]
+def conv_last(table, source, sink, rows, order, ready):
+    channels, width = source.shape[2], source.shape[3]
     tall = table.shape[0] // 3
     lanes = lax.broadcasted_iota(jnp.int32, (tall, width), 1)
     depth = (rows + 2) * 4 * channels
-    group = 2 if planes % 4 == 0 else 1
-    for first in range(0, planes, 2 * group):
-        taken = [
-            source[: rows + 2, first + 2 * k : first + 2 * k + 4].reshape(depth, width) for k in range(group)
-        ]
+    for first in range(0, len(order), 2):
+        targets = order[first : first + 2]
+        taken = [source[: rows + 2, pl.ds(2 * target, 4)].reshape(depth, width) for target in targets]
         product = multiply(table[...], jnp.concatenate(taken, axis=1))
-        for k in range(group):
+        for k, target in enumerate(targets):
             parts = [product[t * tall : (t + 1) * tall, k * width : (k + 1) * width] for t in range(3)]
-            sink[first // 2 + k] = along_z(*parts, lanes).reshape(sink.shape[1:])
+            sink[target] = along_z(*parts, lanes).reshape(sink.shape[1:])
+        for k, target in enumerate(targets):
+            ready(first + k, target)
 
 
 def step_kernel(
-    shares, coils, maps, measured, mask, prior, y_table, z_table, w_first, w_middle, w_last,
-    out, refined,
-    part, outbox, inbox, own_rhs, rhs, own_residual, residual, note, notes, fields, taken_fields,
-    base, first_table, middle_table, last_table, shifted, even, odd, corrections, arrived,
-    block_send, block_recv, note_send, note_recv, edge_send, edge_recv, field_send, field_recv, back_send, back_recv,
+    shares, coils, *refs,
 ):
+    outside, (half, correction), refs = refs[:9], refs[9:11], refs[11:]
+    inside, load_sem, refs = refs[:9], refs[9], refs[10:]
+    maps, measured, mask, prior, y_table, z_table, w_first, w_middle, w_last = inside
+    (
+        part, outbox, inbox, own_rhs, rhs, own_residual, residual, note, notes, fields, taken_fields,
+        base, first_table, middle_table, last_table, shifted, even, odd, corrections, arrived,
+        block_send, block_recv, note_send, note_recv, edge_send, edge_recv, field_send, field_recv, back_send, back_recv,
+    ) = refs
+    loads = [
+        pltpu.make_async_copy(source, target, load_sem.at[index])
+        for index, (source, target) in enumerate(zip(outside, inside))
+    ]
+    for index in (1, 2, 4, 5, 0, 6, 8, 3, 7):
+        loads[index].start()
     slab = lax.axis_index("slab")
     coil = lax.axis_index("coil")
     devices = shares * coils
@@ -273,15 +283,15 @@
         )
 
     def tell(phase):
-        copies = []
         for distance in range(1, devices):
-            copies.append(
-                send(
-                    note.at[phase], notes.at[phase, distance - 1], note_send.at[phase, distance - 1],
-                    note_recv.at[phase, distance - 1], device_at(distance),
-                )
+            send(
+                note.at[phase], notes.at[phase, distance - 1], note_send.at[phase], note_recv.at[phase],
+                device_at(distance),
             )
-        return copies
+        return pltpu.make_async_remote_copy(
+            src_ref=notes.at[phase], dst_ref=notes.at[phase], send_sem=note_send.at[phase],
+            recv_sem=note_recv.at[phase], device_id=device_at(1), device_id_type=MESH,
+        )
 
     def send_edges(which):
         above = lax.rem(coil + coils - 1, coils)
@@ -315,9 +325,12 @@
         taken_fields[which, :, slab + 1] = fields[which, pl.ds(slab * rows, deep)]
         return copies
 
+    sent = []
+
     def finish(copies):
         for copy in copies:
-            copy.wait()
+            copy.wait_recv()
+        sent.extend(copies)
 
     lanes = lax.broadcasted_iota(jnp.int32, (1, note.shape[2]), 1)
 
@@ -360,12 +373,16 @@
         return real, imag
 
     pending = []
+    for index in (1, 2, 4, 5, 0):
+        loads[index].wait()
     for p in range(planes):
         sampled = mask[p].astype(jnp.float32)
         backward_part(measured[0, p] * sampled, measured[1, p] * sampled, 0, p)
         if p == 0:
             pl.semaphore_wait(barrier, devices - 1)
         pending.append(scatter(0, p))
+    for index in (6, 8, 3, 7):
+        loads[index].wait()
     first_weights(w_first, base, first_table)
     last_weights(w_last, last_table, last_table.shape[0] // 12)
     total = taken_fields.shape[2]
@@ -409,7 +426,7 @@
         backward_part(real, imag, 1, p)
         pending.append(scatter(1, p))
     field_copies = send_fields(0, edge_copies)
-    finish(first_notes)
+    first_notes.wait_recv()
     norm, curvature = read_notes(0, 2)
     step = norm / curvature
     gathers = []
@@ -442,7 +459,7 @@
     write_note(1, [norm_next, energy, cross])
     last_notes = tell(1)
     finish(field_copies)
-    finish(last_notes)
+    last_notes.wait_recv()
     norm_next, energy, cross = read_notes(1, 3)
     ratio = norm_next / norm
     curvature = energy + 2.0 * ratio * cross + ratio * ratio * curvature
@@ -461,7 +478,7 @@
             shifted[y, :, group * width : (group + 1) * width] = piece.astype(jnp.bfloat16)
     for h in range(2):
         for p in range(planes):
-            out[h, p] = share * own_rhs[h, p] + step_next * own_residual[h, p]
+            half[h, p] = 0.5 * (share * own_rhs[h, p] + step_next * own_residual[h, p])
     top = coil * block + slab * rows
     left = layers - 1
     conv_first(first_table, shifted, even, rows + 2 * left, top - left, height)
@@ -472,23 +489,32 @@
             middle_table.at[layer], buffers[layer % 2], buffers[(layer + 1) % 2], rows + 2 * left, y_outs,
             top - left, height,
         )
-    conv_last(last_table, buffers[(layers - 2) % 2], corrections, rows)
     copies = []
-    for distance in range(1, shares):
-        other = lax.rem(slab + distance, shares)
-        copies.append(
-            send(
-                corrections.at[other], arrived.at[slab], back_send.at[distance - 1],
-                back_recv.at[distance - 1], (other, coil),
+
+    def give(index, other):
+        if index < shares - 1:
+            copies.append(
+                send(
+                    corrections.at[other], arrived.at[slab], back_send.at[index], back_recv.at[index], (other, coil)
+                )
             )
-        )
+
+    order = [lax.rem(slab + shares - 1 - index, shares) for index in range(shares)]
+    conv_last(last_table, buffers[(layers - 2) % 2], corrections, rows, order, give)
     arrived[slab] = corrections[slab]
+    for copy in sent:
+        copy.wait_send()
+    first_notes.wait_send()
+    last_notes.wait_send()
+    sent.clear()
     finish(copies)
+    for copy in copies:
+        copy.wait_send()
     for s in range(shares):
         span = slice(s * rows, (s + 1) * rows)
         for p in range(planes):
             for h in range(2):
-                refined[h, p, span] = out[h, p, span] + arrived[s, 2 * p + h, :rows]
+                correction[h, p, span] = arrived[s, 2 * p + h, :rows]
 
 
 def body(sensitivity, kspace, sampling, prior_image, w_first, w_middle, w_last):
@@ -516,12 +542,15 @@
     tall = rows + -rows % 8
     deep = rows + 2 * layers
     hidden = (rows + 2 * (layers - 1), whole + 2, channels, width)
+    operands = (maps, measured, sampling, prior_image, y_table, z_table, w_first, w_middle, w_last)
     kernel = pl.pallas_call(
         functools.partial(step_kernel, shares, coils),
-        out_shape=[jax.ShapeDtypeStruct(brick, jnp.float32)] * 2,
-        in_specs=[pl.BlockSpec(memory_space=pltpu.VMEM)] * 9,
+        out_shape=[pltpu.VMEM(brick, jnp.float32)] * 2,
+        in_specs=[pl.BlockSpec(memory_space=pl.ANY)] * 9,
         out_specs=[pl.BlockSpec(memory_space=pltpu.VMEM)] * 2,
-        scratch_shapes=[
+        scratch_shapes=[pltpu.VMEM(operand.shape, operand.dtype) for operand in operands]
+        + [
+            pltpu.SemaphoreType.DMA((len(operands),)),
             pltpu.VMEM((2,) + image, jnp.float32),
             pltpu.VMEM((3, planes, height, width), jnp.int32),
             pltpu.VMEM((3, coils - 1, planes, block, width), jnp.int32),
@@ -544,8 +573,8 @@
             pltpu.VMEM((shares, 2 * planes, tall, width), jnp.float32),
             pltpu.SemaphoreType.DMA((4, planes, coils - 1)),
             pltpu.SemaphoreType.DMA((4, planes, coils - 1)),
-            pltpu.SemaphoreType.DMA((2, shares * coils - 1)),
-            pltpu.SemaphoreType.DMA((2, shares * coils - 1)),
+            pltpu.SemaphoreType.DMA((2,)),
+            pltpu.SemaphoreType.DMA((2,)),
             pltpu.SemaphoreType.DMA((2, 2)),
             pltpu.SemaphoreType.DMA((2, 2)),
             pltpu.SemaphoreType.DMA((2, shares - 1)),
@@ -557,7 +586,9 @@
             collective_id=0, has_side_effects=True, vmem_limit_bytes=56 * 1024 * 1024
         ),
     )
-    return tuple(kernel(maps, measured, sampling, prior_image, y_table, z_table, w_first, w_middle, w_last))
+    half, correction = kernel(*operands)
+    image = half + half
+    return image, image + correction
 
 
 def solution(mesh):

time: 59.6 us -> 55.8 us (0.936)
  local copies, waits for them, and re-layouts: 2.26 us -> 0 us
  Pallas kernels: 56.5 us -> 54.3 us
  other arithmetic: 0 us -> 0.72 us
    unnamed x4 -> x0, local copies, waits for them, and re-layouts: 2.26 us -> none
    pallas_call x1, Pallas kernels: 56.5 us -> 54.3 us  [body(): half, correction = kernel(*operands)]
    add x0 -> x1, other arithmetic: none -> 0.72 us  [body(): return (image, image + correction)]
where the time goes in v3:
time: 55.8 us; the launch traced here: 55.7 us
  Pallas kernels  54.3 us (97%)
  other arithmetic  0.72 us (1%)
  between operations  0.64 us (1%)
    pallas_call x1, Pallas kernels, body(): half, correction = kernel(*operands)  54.3 us

profile of v3, /device:TPU:0, one launch (start us, length us, event | category | flops | bytes accessed | tf_op | source)
XLA Modules:
  0.0 55.7 jit_solution(8553528138886142008)
XLA Ops:
  0.6 54.3 %shard_map.104 = (f32[2,2,64,128]{3,2,1,0:T(8,128)S(1)}, f32[2,2,64,128]{3,2,1,0:T(8,128)S(1)}) custom-call(f32[2,2,256,128]{3,2,1,0:T(8,128)} %bitcast.8, f32[2,2,256,128]{3,2,1,0:T(8,128)} %bitcast.9, s32[2,256,128]{2,1,0:T(8,128)} %refs_2_.1, f32[2,2,64,128]{3,2,1,0:T(8,128)} %refs_3_.1, bf16[512,768]{1,0:T(8,128)(2,1)} %constant.4.clone.refs_4_, ...), custom_call_target="tpu_custom_call" | custom-call | tf_op jit(solution)/shard_map/pallas_call | solution.py:589
  54.9 0.7 %fusion = (f32[2,2,64,128]{3,2,1,0:T(8,128)}, f32[2,2,64,128]{3,2,1,0:T(8,128)}) fusion(f32[2,2,64,128]{3,2,1,0:T(8,128)S(1)} %get-tuple-element.5, f32[2,2,64,128]{3,2,1,0:T(8,128)S(1)} %get-tuple-element.4), kind=kLoop, calls=%fused_computation | loop fusion | flops 65536 | bytes 524288 | tf_op jit(solution)/shard_map/add | solution.py:591

commit v4 on v3

--- a/solution.py
+++ b/solution.py
@@ -37,13 +37,23 @@
 def transform(real, imag, y_table, z_table):
     rows, width = real.shape
     high, low = split(jnp.concatenate([real, imag], axis=1))
-    field = multiply(y_table[...], jnp.concatenate([high, low, high], axis=0))
+    y_high, y_low = y_table[:, :rows], y_table[:, rows:]
+    z_high, z_low = z_table[: 2 * width], z_table[2 * width :]
+    field = multiply(
+        jnp.concatenate([y_high, y_high, y_low], axis=1), jnp.concatenate([high, low, high], axis=0)
+    )
     field = jnp.concatenate(
         [field[:rows, :width] + field[rows:, width:], field[:rows, width:] - field[rows:, :width]], axis=1
     )
     high, low = split(field)
-    field = multiply(jnp.concatenate([high, low, high], axis=1), z_table[...])
+    field = multiply(
+        jnp.concatenate([high, low, high], axis=1), jnp.concatenate([z_high, z_high, z_low], axis=0)
+    )
     return field[:, :width], field[:, width:]
+
+
+def fold(values):
+    return jnp.sum(values.reshape(values.shape[0] // 8, 8, values.shape[1]), axis=0)
 
 
 def total_of(values):
@@ -210,7 +220,7 @@
     inside, load_sem, refs = refs[:9], refs[9], refs[10:]
     maps, measured, mask, prior, y_table, z_table, w_first, w_middle, w_last = inside
     (
-        part, outbox, inbox, own_rhs, rhs, own_residual, residual, note, notes, fields, taken_fields,
+        part, outbox, inbox, own_rhs, rhs, own_image, residual, note, notes, fields, taken_fields,
         base, first_table, middle_table, last_table, shifted, even, odd, corrections, arrived,
         block_send, block_recv, note_send, note_recv, edge_send, edge_recv, field_send, field_recv, back_send, back_recv,
     ) = refs
@@ -223,7 +233,6 @@
     slab = lax.axis_index("slab")
     coil = lax.axis_index("coil")
     devices = shares * coils
-    me = slab * coils + coil
     planes = maps.shape[1]
     height, width = maps.shape[2:]
     block = prior.shape[2]
@@ -233,9 +242,12 @@
     y_outs = 2 if rows % 2 == 0 else 1
     tables = (y_table, z_table)
 
+    offsets = [(s, c) for s in range(shares) for c in range(coils) if s or c]
+    offsets.sort(key=lambda offset: -min(offset[1], coils - offset[1]) - bin(offset[0] // 2).count("1"))
+
     def device_at(distance):
-        other = lax.rem(me + distance, devices)
-        return (other // coils, lax.rem(other, coils))
+        far_slab, far_coil = offsets[distance - 1]
+        return (lax.rem(slab + far_slab, shares), lax.rem(coil + far_coil, coils))
 
     barrier = pltpu.get_barrier_semaphore()
     for distance in range(1, devices):
@@ -272,14 +284,10 @@
             lambda distance: inbox.at[phase, distance - 1, p],
         )
 
-    def gather_rhs(p):
+    def gather(phase, p):
         return to_coils(
-            2, p, lambda other: outbox.at[2, p, pl.ds(0, block)], lambda distance: inbox.at[2, distance - 1, p]
-        )
-
-    def gather(p):
-        return to_coils(
-            3, p, lambda other: residual.at[:, p, mine], lambda distance: residual.at[:, p, mine]
+            phase, p, lambda other: outbox.at[phase, p, pl.ds(0, block)],
+            lambda distance: inbox.at[phase, distance - 1, p],
         )
 
     def tell(phase):
@@ -394,19 +402,19 @@
         for outer in (0, buffer.shape[1] - 1):
             buffer[:, outer] = jnp.zeros((buffer.shape[0],) + buffer.shape[2:], buffer.dtype)
     gathers = []
-    norm = jnp.zeros((1, 1), jnp.float32)
+    norm = jnp.zeros((8, width), jnp.float32)
     for p in range(planes):
         finish(pending[p])
         real, imag = reduced(0, p)
         real = real + LAMBDA * prior[0, p]
         imag = imag + LAMBDA * prior[1, p]
         outbox[2, p, :block] = pack(real, imag)
-        gathers.append(gather_rhs(p))
+        gathers.append(gather(2, p))
         for h, value in enumerate((real, imag)):
             own_rhs[h, p] = value
             rhs[h, p, mine] = value
             fields[0, halo : halo + block, 2 * p + h] = value
-            norm = norm + total_of(value * value)
+            norm = norm + fold(value * value)
     edge_copies = send_edges(0)
     middle_weights(w_middle, middle_table, y_outs)
     energy = LAMBDA * norm
@@ -419,44 +427,51 @@
             rhs[0, p, source] = real
             rhs[1, p, source] = imag
         real, imag = forward(rhs[0, p], rhs[1, p], p)
-        energy = energy + total_of(real * real) + total_of(imag * imag)
-        if p == planes - 1:
-            write_note(0, [norm, energy])
-            first_notes = tell(0)
+        energy = energy + fold(real * real + imag * imag)
         backward_part(real, imag, 1, p)
         pending.append(scatter(1, p))
+    write_note(0, [total_of(norm), total_of(energy)])
+    first_notes = tell(0)
     field_copies = send_fields(0, edge_copies)
+    gathers = []
+    for p in range(planes):
+        finish(pending[p])
+        images = reduced(1, p)
+        images = [images[h] + LAMBDA * own_rhs[h, p] for h in range(2)]
+        outbox[3, p, :block] = pack(*images)
+        if p < planes - 1:
+            gathers.append(gather(3, p))
+        for h in range(2):
+            own_image[h, p] = images[h]
+            fields[1, halo : halo + block, 2 * p + h] = images[h]
+    edge_copies = send_edges(1)
+    gathers.append(gather(3, planes - 1))
     first_notes.wait_recv()
     norm, curvature = read_notes(0, 2)
     step = norm / curvature
-    gathers = []
-    norm_next = jnp.zeros((1, 1), jnp.float32)
-    cross = jnp.zeros((1, 1), jnp.float32)
+    norm_next = jnp.zeros((8, width), jnp.float32)
+    cross = jnp.zeros((8, width), jnp.float32)
     for p in range(planes):
-        finish(pending[p])
-        images = reduced(1, p)
         for h in range(2):
-            direction = own_rhs[h, p]
-            image = images[h] + LAMBDA * direction
-            value = direction - step * image
-            own_residual[h, p] = value
-            residual[h, p, mine] = value.astype(jnp.bfloat16)
-            fields[1, halo : halo + block, 2 * p + h] = value
-        gathers.append(gather(p))
-        for h in range(2):
-            value = own_residual[h, p]
-            image = images[h] + LAMBDA * own_rhs[h, p]
-            norm_next = norm_next + total_of(value * value)
-            cross = cross + total_of(value * image)
-    edge_copies = send_edges(1)
+            image = own_image[h, p]
+            value = own_rhs[h, p] - step * image
+            norm_next = norm_next + fold(value * value)
+            cross = cross + fold(value * image)
     energy = LAMBDA * norm_next
+    norm_next, cross = total_of(norm_next), total_of(cross)
     for p in range(planes):
         finish(gathers[p])
-        if p == planes - 1:
+        if p == 0:
             field_copies = field_copies + send_fields(1, edge_copies)
-        real, imag = forward(residual[0, p].astype(jnp.float32), residual[1, p].astype(jnp.float32), p)
-        energy = energy + total_of(real * real) + total_of(imag * imag)
-    write_note(1, [norm_next, energy, cross])
+        for h in range(2):
+            residual[h, mine] = own_rhs[h, p] - step * own_image[h, p]
+        for distance in range(1, coils):
+            source = rows_of(lax.rem(coil + coils - distance, coils))
+            for h, value in enumerate(unpack(inbox[3, distance - 1, p])):
+                residual[h, source] = rhs[h, p, source] - step * value
+        real, imag = forward(residual[0], residual[1], p)
+        energy = energy + fold(real * real + imag * imag)
+    write_note(1, [norm_next, total_of(energy), cross])
     last_notes = tell(1)
     finish(field_copies)
     last_notes.wait_recv()
@@ -464,11 +479,12 @@
     ratio = norm_next / norm
     curvature = energy + 2.0 * ratio * cross + ratio * ratio * curvature
     step_next = norm_next / curvature
-    share = step + step_next * ratio
+    share = step + step_next * (1.0 + ratio)
+    share_image = -step_next * step
     across = lax.broadcasted_iota(jnp.int32, (4 * total, width), 1)
     for y in range(deep):
         line = share * taken_fields[0, y].reshape(4 * total, width)
-        line = line + step_next * taken_fields[1, y].reshape(4 * total, width)
+        line = line + share_image * taken_fields[1, y].reshape(4 * total, width)
         line = line.astype(jnp.bfloat16).astype(jnp.float32)
         before = jnp.where(across == 0, 0.0, pltpu.roll(line, 1, 1))
         after = jnp.where(across == width - 1, 0.0, pltpu.roll(line, width - 1, 1))
@@ -478,7 +494,7 @@
             shifted[y, :, group * width : (group + 1) * width] = piece.astype(jnp.bfloat16)
     for h in range(2):
         for p in range(planes):
-            half[h, p] = 0.5 * (share * own_rhs[h, p] + step_next * own_residual[h, p])
+            half[h, p] = 0.5 * (share * own_rhs[h, p] + share_image * own_image[h, p])
     top = coil * block + slab * rows
     left = layers - 1
     conv_first(first_table, shifted, even, rows + 2 * left, top - left, height)
@@ -530,10 +546,10 @@
     y_outs = 2 if rows % 2 == 0 else 1
     cosine, sine = dft_parts(height)
     high, low = halves(np.concatenate([cosine, sine]))
-    y_table = np.concatenate([high, high, low], axis=1)
+    y_table = np.concatenate([high, low], axis=1)
     cosine, sine = dft_parts(width)
     high, low = halves(np.block([[cosine, -sine], [sine, cosine]]))
-    z_table = np.concatenate([high, high, low], axis=0)
+    z_table = np.concatenate([high, low], axis=0)
     w_first = jnp.transpose(w_first, (2, 3, 4, 1, 0))
     w_middle = jnp.transpose(w_middle, (0, 3, 4, 5, 1, 2)).reshape(layers - 2, 3, 3, 3 * channels, channels)
     w_last = jnp.transpose(w_last, (2, 3, 4, 0, 1))
@@ -552,12 +568,12 @@
         + [
             pltpu.SemaphoreType.DMA((len(operands),)),
             pltpu.VMEM((2,) + image, jnp.float32),
-            pltpu.VMEM((3, planes, height, width), jnp.int32),
-            pltpu.VMEM((3, coils - 1, planes, block, width), jnp.int32),
+            pltpu.VMEM((4, planes, height, width), jnp.int32),
+            pltpu.VMEM((4, coils - 1, planes, block, width), jnp.int32),
             pltpu.VMEM(brick, jnp.float32),
             pltpu.VMEM(image, jnp.float32),
             pltpu.VMEM(brick, jnp.float32),
-            pltpu.VMEM(image, jnp.bfloat16),
+            pltpu.VMEM((2, height, width), jnp.float32),
             pltpu.VMEM((2, 1, 128), jnp.float32),
             pltpu.VMEM((2, shares * coils - 1, 1, 128), jnp.float32),
             pltpu.VMEM((2, block + 2 * layers, 2 * planes, width), jnp.float32),

time: 55.8 us -> 53.8 us (0.964)
  Pallas kernels: 54.3 us -> 52.3 us
    pallas_call x1, Pallas kernels: 54.3 us -> 52.3 us  [body(): half, correction = kernel(*operands)]
where the time goes in v4:
time: 53.8 us; the launch traced here: 53.7 us
  Pallas kernels  52.3 us (97%)
  other arithmetic  0.72 us (1%)
  between operations  0.64 us (1%)
    pallas_call x1, Pallas kernels, body(): half, correction = kernel(*operands)  52.3 us

profile of v4, /device:TPU:0, one launch (start us, length us, event | category | flops | bytes accessed | tf_op | source)
XLA Modules:
  0.0 53.7 jit_solution(8060631238909900151)
XLA Ops:
  0.6 52.3 %shard_map.104 = (f32[2,2,64,128]{3,2,1,0:T(8,128)S(1)}, f32[2,2,64,128]{3,2,1,0:T(8,128)S(1)}) custom-call(f32[2,2,256,128]{3,2,1,0:T(8,128)} %bitcast.8, f32[2,2,256,128]{3,2,1,0:T(8,128)} %bitcast.9, s32[2,256,128]{2,1,0:T(8,128)} %refs_2_.1, f32[2,2,64,128]{3,2,1,0:T(8,128)} %refs_3_.1, bf16[512,512]{1,0:T(8,128)(2,1)} %constant.4.clone.refs_4_, ...), custom_call_target="tpu_custom_call" | custom-call | tf_op jit(solution)/shard_map/pallas_call | solution.py:605
  53.0 0.7 %fusion = (f32[2,2,64,128]{3,2,1,0:T(8,128)}, f32[2,2,64,128]{3,2,1,0:T(8,128)}) fusion(f32[2,2,64,128]{3,2,1,0:T(8,128)S(1)} %get-tuple-element.5, f32[2,2,64,128]{3,2,1,0:T(8,128)S(1)} %get-tuple-element.4), kind=kLoop, calls=%fused_computation | loop fusion | flops 65536 | bytes 524288 | tf_op jit(solution)/shard_map/add | solution.py:607

commit v5 on v4

--- a/solution.py
+++ b/solution.py
@@ -95,13 +95,13 @@
     return jnp.concatenate([empty] * x_out + blocks + [empty] * (1 - x_out), axis=1)
 
 
-def first_weights(taps, base, table):
+def first_weights(taps, base, table, mirrored):
     outs = taps.shape[-1]
     for u in range(3):
         for v in range(3):
             for t in range(3):
                 index = ((v * 3 + t) * 3 + u) * 2
-                base[index : index + 2, :outs] = taps[u, v, t].astype(jnp.float32)
+                base[index : index + 2, :outs] = taps[u, jnp.where(mirrored, 2 - v, v), t].astype(jnp.float32)
     window = (24, table.shape[0])
     row = lax.broadcasted_iota(jnp.int32, window, 0)
     place = row - 2 * (lax.broadcasted_iota(jnp.int32, window, 1) // outs) - 2
@@ -120,21 +120,21 @@
     table[...] = jnp.transpose(jnp.concatenate(blocks, axis=0)).astype(table.dtype)
 
 
-def middle_weights(taps, table, y_outs):
+def middle_weights(taps, table, y_outs, mirrored):
     count, channels = taps.shape[3:]
     span = 4 * channels
     table[...] = jnp.zeros(table.shape, table.dtype)
     for layer in range(taps.shape[0]):
         for v in range(3):
             for x_out in range(2):
-                block = spread([taps[layer, u, v] for u in range(3)], x_out)
+                block = spread([taps[layer, u, jnp.where(mirrored, 2 - v, v)] for u in range(3)], x_out)
                 for y_out in range(y_outs):
                     base = (x_out * y_outs + y_out) * count
                     y_in = y_out + v
                     table[layer, base : base + count, y_in * span : (y_in + 1) * span] = block
 
 
-def last_weights(taps, table, tall):
+def last_weights(taps, table, tall, mirrored):
     channels = taps.shape[-1]
     span = 4 * channels
     row = lax.broadcasted_iota(jnp.int32, (tall, span), 0)
@@ -143,11 +143,13 @@
             lines = [spread([taps[u, v, t].astype(jnp.float32) for u in range(3)], x_out) for v in range(3)]
             for o in range(2):
                 base = ((t * 2 + x_out) * 2 + o) * tall
-                for y_in in range(table.shape[1] // span):
+                count = table.shape[1] // span
+                for index in range(count):
+                    y_in = jnp.where(mirrored, count - 1 - index, index)
                     block = jnp.zeros((tall, span), jnp.float32)
                     for v in range(3):
                         block = jnp.where(row == y_in - v, lines[v][o : o + 1], block)
-                    table[base : base + tall, y_in * span : (y_in + 1) * span] = block.astype(table.dtype)
+                    table[base : base + tall, index * span : (index + 1) * span] = block.astype(table.dtype)
 
 
 def along_z(before, centre, after, lanes):
@@ -157,44 +159,53 @@
     return centre + before + after
 
 
-def conv_first(table, taken, sink, rows, top, height):
+def conv_first(table, taken, sink, rows, inside, ready):
     outs = sink.shape[2]
     width = sink.shape[3]
     depth = 3 * taken.shape[1]
     for y in range(rows):
-        inside = jnp.logical_and(top + y >= 0, top + y < height)
         product = multiply(table[:, :depth], taken[y : y + 3].reshape(depth, taken.shape[2]))
         for group in range(taken.shape[2] // width):
             for q in range(table.shape[0] // outs):
                 value = product[q * outs : (q + 1) * outs, group * width : (group + 1) * width]
-                value = jnp.where(inside, jnp.maximum(value, 0.0), 0.0)
-                sink[y, group * (table.shape[0] // outs) + q + 1] = value.astype(jnp.bfloat16)
-
-
-def conv_middle(table, source, sink, rows, y_outs, top, height):
+                value = jnp.where(inside(y), jnp.maximum(value, 0.0), 0.0)
+                sink[y + 1, group * (table.shape[0] // outs) + q + 1] = value.astype(jnp.bfloat16)
+        if y == 0:
+            ready()
+
+
+def conv_middle(table, source, sink, rows, y_outs, inside, ready):
     planes, outs, width = source.shape[1] - 2, source.shape[2], source.shape[3]
     lanes = lax.broadcasted_iota(jnp.int32, (outs, width), 1)
-    depth = (y_outs + 2) * 4 * outs
     group = 2 if planes % 4 == 0 else 1
     for y in range(0, rows, y_outs):
+        tall = min(y_outs, rows - y)
+        depth = (tall + 2) * 4 * outs
+        if tall == y_outs:
+            weights = table[...]
+        else:
+            step = 3 * outs
+            weights = [table[x * y_outs * step : (x * y_outs + tall) * step, :depth] for x in range(2)]
+            weights = jnp.concatenate(weights, axis=0)
         for first in range(0, planes, 2 * group):
             taken = [
-                source[y : y + y_outs + 2, first + 2 * k : first + 2 * k + 4].reshape(depth, width)
+                source[y : y + tall + 2, first + 2 * k : first + 2 * k + 4].reshape(depth, width)
                 for k in range(group)
             ]
-            product = multiply(table[...], jnp.concatenate(taken, axis=1))
+            product = multiply(weights, jnp.concatenate(taken, axis=1))
             for x_out in range(2):
-                for y_out in range(y_outs):
-                    base = (x_out * y_outs + y_out) * 3 * outs
-                    inside = jnp.logical_and(top + y + y_out >= 0, top + y + y_out < height)
+                for y_out in range(tall):
+                    base = (x_out * tall + y_out) * 3 * outs
                     for k in range(group):
                         parts = [
                             product[base + t * outs : base + (t + 1) * outs, k * width : (k + 1) * width]
                             for t in range(3)
                         ]
                         value = along_z(*parts, lanes)
-                        value = jnp.where(inside, jnp.maximum(value, 0.0), 0.0)
-                        sink[y + y_out, first + 2 * k + x_out + 1] = value.astype(jnp.bfloat16)
+                        value = jnp.where(inside(y + y_out), jnp.maximum(value, 0.0), 0.0)
+                        sink[y + y_out + 1, first + 2 * k + x_out + 1] = value.astype(jnp.bfloat16)
+        if y == 0:
+            ready()
 
 
 def conv_last(table, source, sink, rows, order, ready):
@@ -221,8 +232,9 @@
     maps, measured, mask, prior, y_table, z_table, w_first, w_middle, w_last = inside
     (
         part, outbox, inbox, own_rhs, rhs, own_image, residual, note, notes, fields, taken_fields,
-        base, first_table, middle_table, last_table, shifted, even, odd, corrections, arrived,
+        base, first_table, middle_table, last_table, shifted, corrections, arrived,
         block_send, block_recv, note_send, note_recv, edge_send, edge_recv, field_send, field_recv, back_send, back_recv,
+        pair_send, pair_recv, *hidden,
     ) = refs
     loads = [
         pltpu.make_async_copy(source, target, load_sem.at[index])
@@ -391,14 +403,15 @@
         pending.append(scatter(0, p))
     for index in (6, 8, 3, 7):
         loads[index].wait()
-    first_weights(w_first, base, first_table)
-    last_weights(w_last, last_table, last_table.shape[0] // 12)
+    mirrored = lax.rem(slab, 2) == 0
+    first_weights(w_first, base, first_table, mirrored)
+    last_weights(w_last, last_table, last_table.shape[0] // 12, mirrored)
     total = taken_fields.shape[2]
     for which in range(2):
         for outer in (0, total - 1):
             taken_fields[which, :, outer] = jnp.zeros((deep,) + taken_fields.shape[3:], jnp.float32)
     shifted[...] = jnp.zeros(shifted.shape, shifted.dtype)
-    for buffer in (even, odd):
+    for buffer in hidden:
         for outer in (0, buffer.shape[1] - 1):
             buffer[:, outer] = jnp.zeros((buffer.shape[0],) + buffer.shape[2:], buffer.dtype)
     gathers = []
@@ -416,7 +429,7 @@
             fields[0, halo : halo + block, 2 * p + h] = value
             norm = norm + fold(value * value)
     edge_copies = send_edges(0)
-    middle_weights(w_middle, middle_table, y_outs)
+    middle_weights(w_middle, middle_table, y_outs, mirrored)
     energy = LAMBDA * norm
     pending = []
     for p in range(planes):
@@ -461,8 +474,6 @@
     norm_next, cross = total_of(norm_next), total_of(cross)
     for p in range(planes):
         finish(gathers[p])
-        if p == 0:
-            field_copies = field_copies + send_fields(1, edge_copies)
         for h in range(2):
             residual[h, mine] = own_rhs[h, p] - step * own_image[h, p]
         for distance in range(1, coils):
@@ -471,6 +482,8 @@
                 residual[h, source] = rhs[h, p, source] - step * value
         real, imag = forward(residual[0], residual[1], p)
         energy = energy + fold(real * real + imag * imag)
+        if p == 0:
+            field_copies = field_copies + send_fields(1, edge_copies)
     write_note(1, [norm_next, total_of(energy), cross])
     last_notes = tell(1)
     finish(field_copies)
@@ -482,7 +495,8 @@
     share = step + step_next * (1.0 + ratio)
     share_image = -step_next * step
     across = lax.broadcasted_iota(jnp.int32, (4 * total, width), 1)
-    for y in range(deep):
+    for index in range(shifted.shape[0]):
+        y = jnp.where(mirrored, rows + halo - index, halo - 1 + index)
         line = share * taken_fields[0, y].reshape(4 * total, width)
         line = line + share_image * taken_fields[1, y].reshape(4 * total, width)
         line = line.astype(jnp.bfloat16).astype(jnp.float32)
@@ -491,20 +505,32 @@
         for group in range(shifted.shape[2] // width):
             span = slice(16 * group, 16 * group + 24)
             piece = jnp.concatenate([before[span], line[span], after[span], jnp.zeros((8, width), jnp.float32)], axis=0)
-            shifted[y, :, group * width : (group + 1) * width] = piece.astype(jnp.bfloat16)
+            shifted[index, :, group * width : (group + 1) * width] = piece.astype(jnp.bfloat16)
     for h in range(2):
         for p in range(planes):
             half[h, p] = 0.5 * (share * own_rhs[h, p] + share_image * own_image[h, p])
     top = coil * block + slab * rows
-    left = layers - 1
-    conv_first(first_table, shifted, even, rows + 2 * left, top - left, height)
-    buffers = (even, odd)
+    partner = slab + 1 - 2 * lax.rem(slab, 2)
+    exchanged = []
+
+    def inside(m):
+        y = top + jnp.where(mirrored, rows - 1 - m, m)
+        return jnp.logical_and(y >= 0, y < height)
+
+    def share_row(layer):
+        buffer = hidden[layer]
+        exchanged.append(
+            send(buffer.at[1], buffer.at[0], pair_send.at[layer], pair_recv.at[layer], (partner, coil))
+        )
+
+    conv_first(first_table, shifted, hidden[0], rows + layers - 1, inside, lambda: share_row(0))
     for layer in range(layers - 2):
-        left = left - 1
+        finish(exchanged[-1:])
         conv_middle(
-            middle_table.at[layer], buffers[layer % 2], buffers[(layer + 1) % 2], rows + 2 * left, y_outs,
-            top - left, height,
+            middle_table.at[layer], hidden[layer], hidden[layer + 1], rows + layers - 2 - layer, y_outs, inside,
+            lambda: share_row(layer + 1),
         )
+    finish(exchanged[-1:])
     copies = []
 
     def give(index, other):
@@ -516,7 +542,7 @@
             )
 
     order = [lax.rem(slab + shares - 1 - index, shares) for index in range(shares)]
-    conv_last(last_table, buffers[(layers - 2) % 2], corrections, rows, order, give)
+    conv_last(last_table, hidden[layers - 2], corrections, rows, order, give)
     arrived[slab] = corrections[slab]
     for copy in sent:
         copy.wait_send()
@@ -557,7 +583,6 @@
     brick = (2, planes, block, width)
     tall = rows + -rows % 8
     deep = rows + 2 * layers
-    hidden = (rows + 2 * (layers - 1), whole + 2, channels, width)
     operands = (maps, measured, sampling, prior_image, y_table, z_table, w_first, w_middle, w_last)
     kernel = pl.pallas_call(
         functools.partial(step_kernel, shares, coils),
@@ -582,9 +607,7 @@
             pltpu.VMEM((8 * channels, 256), jnp.bfloat16),
             pltpu.VMEM((layers - 2, 2 * y_outs * 3 * channels, (y_outs + 2) * 4 * channels), jnp.bfloat16),
             pltpu.VMEM((12 * tall, (rows + 2) * 4 * channels), jnp.bfloat16),
-            pltpu.VMEM((deep, 80, whole // 8 * width), jnp.bfloat16),
-            pltpu.VMEM(hidden, jnp.bfloat16),
-            pltpu.VMEM(hidden, jnp.bfloat16),
+            pltpu.VMEM((rows + layers + 1, 80, whole // 8 * width), jnp.bfloat16),
             pltpu.VMEM((shares, 2 * planes, tall, width), jnp.float32),
             pltpu.VMEM((shares, 2 * planes, tall, width), jnp.float32),
             pltpu.SemaphoreType.DMA((4, planes, coils - 1)),
@@ -597,6 +620,12 @@
             pltpu.SemaphoreType.DMA((2, shares - 1)),
             pltpu.SemaphoreType.DMA((shares - 1,)),
             pltpu.SemaphoreType.DMA((shares - 1,)),
+            pltpu.SemaphoreType.DMA((layers - 1,)),
+            pltpu.SemaphoreType.DMA((layers - 1,)),
+        ]
+        + [
+            pltpu.VMEM((rows + layers - layer, whole + 2, channels, width), jnp.bfloat16)
+            for layer in range(layers - 1)
         ],
         compiler_params=pltpu.CompilerParams(
             collective_id=0, has_side_effects=True, vmem_limit_bytes=56 * 1024 * 1024

time: 53.8 us -> 54.7 us (1.017)
  Pallas kernels: 52.3 us -> 53.2 us
    pallas_call x1, Pallas kernels: 52.3 us -> 53.2 us  [body(): half, correction = kernel(*operands)]
where the time goes in v5:
time: 54.7 us; the launch traced here: 54.5 us
  Pallas kernels  53.2 us (97%)
  other arithmetic  0.72 us (1%)
  between operations  0.64 us (1%)
    pallas_call x1, Pallas kernels, body(): half, correction = kernel(*operands)  53.2 us

profile of v5, /device:TPU:0, one launch (start us, length us, event | category | flops | bytes accessed | tf_op | source)
XLA Modules:
  0.0 54.5 jit_solution(115910915453576814)
XLA Ops:
  0.6 53.2 %shard_map.104 = (f32[2,2,64,128]{3,2,1,0:T(8,128)S(1)}, f32[2,2,64,128]{3,2,1,0:T(8,128)S(1)}) custom-call(f32[2,2,256,128]{3,2,1,0:T(8,128)} %bitcast.8, f32[2,2,256,128]{3,2,1,0:T(8,128)} %bitcast.9, s32[2,256,128]{2,1,0:T(8,128)} %refs_2_.1, f32[2,2,64,128]{3,2,1,0:T(8,128)} %refs_3_.1, bf16[512,512]{1,0:T(8,128)(2,1)} %constant.4.clone.refs_4_, ...), custom_call_target="tpu_custom_call" | custom-call | tf_op jit(solution)/shard_map/pallas_call | solution.py:634
  53.8 0.7 %fusion = (f32[2,2,64,128]{3,2,1,0:T(8,128)}, f32[2,2,64,128]{3,2,1,0:T(8,128)}) fusion(f32[2,2,64,128]{3,2,1,0:T(8,128)S(1)} %get-tuple-element.5, f32[2,2,64,128]{3,2,1,0:T(8,128)S(1)} %get-tuple-element.4), kind=kLoop, calls=%fused_computation | loop fusion | flops 65536 | bytes 524288 | tf_op jit(solution)/shard_map/add | solution.py:636

commit v6 on v4

--- a/solution.py
+++ b/solution.py
@@ -228,8 +228,6 @@
         pltpu.make_async_copy(source, target, load_sem.at[index])
         for index, (source, target) in enumerate(zip(outside, inside))
     ]
-    for index in (1, 2, 4, 5, 0, 6, 8, 3, 7):
-        loads[index].start()
     slab = lax.axis_index("slab")
     coil = lax.axis_index("coil")
     devices = shares * coils
@@ -252,6 +250,9 @@
     barrier = pltpu.get_barrier_semaphore()
     for distance in range(1, devices):
         pl.semaphore_signal(barrier, inc=1, device_id=device_at(distance), device_id_type=MESH)
+
+    for index in (1, 2, 4, 5, 0, 6, 8, 3, 7):
+        loads[index].start()
 
     def rows_of(index):
         return pl.ds(pl.multiple_of(index * block, block), block)
@@ -461,8 +462,6 @@
     norm_next, cross = total_of(norm_next), total_of(cross)
     for p in range(planes):
         finish(gathers[p])
-        if p == 0:
-            field_copies = field_copies + send_fields(1, edge_copies)
         for h in range(2):
             residual[h, mine] = own_rhs[h, p] - step * own_image[h, p]
         for distance in range(1, coils):
@@ -471,6 +470,8 @@
                 residual[h, source] = rhs[h, p, source] - step * value
         real, imag = forward(residual[0], residual[1], p)
         energy = energy + fold(real * real + imag * imag)
+        if p == 0:
+            field_copies = field_copies + send_fields(1, edge_copies)
     write_note(1, [norm_next, total_of(energy), cross])
     last_notes = tell(1)
     finish(field_copies)

time: 53.8 us -> 53.8 us (level)
  no operation moved by 1% of the time
where the time goes in v6:
time: 53.8 us; the launch traced here: 53.7 us
  Pallas kernels  52.3 us (97%)
  other arithmetic  0.72 us (1%)
  between operations  0.64 us (1%)
    pallas_call x1, Pallas kernels, body(): half, correction = kernel(*operands)  52.3 us

profile of v6, /device:TPU:0, one launch (start us, length us, event | category | flops | bytes accessed | tf_op | source)
XLA Modules:
  0.0 53.7 jit_solution(7529431525457871930)
XLA Ops:
  0.6 52.3 %shard_map.104 = (f32[2,2,64,128]{3,2,1,0:T(8,128)S(1)}, f32[2,2,64,128]{3,2,1,0:T(8,128)S(1)}) custom-call(f32[2,2,256,128]{3,2,1,0:T(8,128)} %bitcast.8, f32[2,2,256,128]{3,2,1,0:T(8,128)} %bitcast.9, s32[2,256,128]{2,1,0:T(8,128)} %refs_2_.1, f32[2,2,64,128]{3,2,1,0:T(8,128)} %refs_3_.1, bf16[512,512]{1,0:T(8,128)(2,1)} %constant.4.clone.refs_4_, ...), custom_call_target="tpu_custom_call" | custom-call | tf_op jit(solution)/shard_map/pallas_call | solution.py:606
  52.9 0.7 %fusion = (f32[2,2,64,128]{3,2,1,0:T(8,128)}, f32[2,2,64,128]{3,2,1,0:T(8,128)}) fusion(f32[2,2,64,128]{3,2,1,0:T(8,128)S(1)} %get-tuple-element.5, f32[2,2,64,128]{3,2,1,0:T(8,128)S(1)} %get-tuple-element.4), kind=kLoop, calls=%fused_computation | loop fusion | flops 65536 | bytes 524288 | tf_op jit(solution)/shard_map/add | solution.py:608

commit v7 on v6

--- a/solution.py
+++ b/solution.py
@@ -462,6 +462,8 @@
     norm_next, cross = total_of(norm_next), total_of(cross)
     for p in range(planes):
         finish(gathers[p])
+        if p == 0:
+            field_copies = field_copies + send_fields(1, edge_copies)
         for h in range(2):
             residual[h, mine] = own_rhs[h, p] - step * own_image[h, p]
         for distance in range(1, coils):
@@ -470,8 +472,6 @@
                 residual[h, source] = rhs[h, p, source] - step * value
         real, imag = forward(residual[0], residual[1], p)
         energy = energy + fold(real * real + imag * imag)
-        if p == 0:
-            field_copies = field_copies + send_fields(1, edge_copies)
     write_note(1, [norm_next, total_of(energy), cross])
     last_notes = tell(1)
     finish(field_copies)

time: 53.8 us -> 53.8 us (level)
  no operation moved by 1% of the time
where the time goes in v7:
time: 53.8 us; the launch traced here: 53.7 us
  Pallas kernels  52.3 us (97%)
  other arithmetic  0.72 us (1%)
  between operations  0.64 us (1%)
    pallas_call x1, Pallas kernels, body(): half, correction = kernel(*operands)  52.3 us

profile of v7, /device:TPU:0, one launch (start us, length us, event | category | flops | bytes accessed | tf_op | source)
XLA Modules:
  0.0 53.7 jit_solution(18232259381316752656)
XLA Ops:
  0.6 52.3 %shard_map.104 = (f32[2,2,64,128]{3,2,1,0:T(8,128)S(1)}, f32[2,2,64,128]{3,2,1,0:T(8,128)S(1)}) custom-call(f32[2,2,256,128]{3,2,1,0:T(8,128)} %bitcast.8, f32[2,2,256,128]{3,2,1,0:T(8,128)} %bitcast.9, s32[2,256,128]{2,1,0:T(8,128)} %refs_2_.1, f32[2,2,64,128]{3,2,1,0:T(8,128)} %refs_3_.1, bf16[512,512]{1,0:T(8,128)(2,1)} %constant.4.clone.refs_4_, ...), custom_call_target="tpu_custom_call" | custom-call | tf_op jit(solution)/shard_map/pallas_call | solution.py:606
  52.9 0.7 %fusion = (f32[2,2,64,128]{3,2,1,0:T(8,128)}, f32[2,2,64,128]{3,2,1,0:T(8,128)}) fusion(f32[2,2,64,128]{3,2,1,0:T(8,128)S(1)} %get-tuple-element.5, f32[2,2,64,128]{3,2,1,0:T(8,128)S(1)} %get-tuple-element.4), kind=kLoop, calls=%fused_computation | loop fusion | flops 65536 | bytes 524288 | tf_op jit(solution)/shard_map/add | solution.py:608
